TPU v7x, 512 devices: a whole 4x8x8 slice. The times are simulated.
512 devices in a mesh: seq: 64 (over z, x, core), chan: 8 (over y).
Axes of the slice: x: 4, y: 8, z: 8, core: 2. Of those that a mesh axis runs over, the one named last changes fastest.
Arguments:
- inner_acts: bfloat16 [32768, 4096], P('seq', 'chan')
- gate_input: bfloat16 [32768, 4096], P('seq', 'chan'), may hold values from -6 to 6
- forward_keys: bfloat16 [32768, 128], P('seq'), may hold values from -0.5 to 0.5
- forward_queries: bfloat16 [32768, 128], P('seq'), may hold values from -6 to 6
- backward_keys: bfloat16 [32768, 128], P('seq'), may hold values from -0.5 to 0.5
- backward_queries: bfloat16 [32768, 128], P('seq'), may hold values from -6 to 6
- decay_codes: int32 [2, 128, 64], P(None, 'seq', 'chan'), may hold values from 1 to 98304
- clip_start: int32 [32768], P('seq'), may hold values 0 or 1
- skip_gain: float32 [64], P('chan'), may hold values from 0.3 to 3
- norm_gain: float32 [4096], P('chan'), may hold values from 0.1 to 1.9
- out_weight: bfloat16 [4096, 2048], P('chan'), may hold values from -0.09375 to 0.09375
Outputs:
- mixed: bfloat16 [8192, 2048], P('seq')
All inputs are finite; a program needn't handle non-finite values. No bound on the sum of `clip_start` on one device may be relied on, other than what follows from the above.
Results may differ from a plain program's by a relative error of at most 0.01.
Values may be sent and summed in bfloat16 or wider, within the bound.
A program may use at most 128 MiB of HBM per device.

v0:
```python
import jax
import jax.numpy as jnp
from jax import lax
from jax.sharding import Mesh
from jax.sharding import PartitionSpec as P

E = 4096
SPAN = 256
POOL = 4
SEQ = ("seq_0", "seq_1", "seq_2")


def neutral_like(x, identity):
    return jax.tree.map(
        lambda part, zero: jnp.zeros_like(part) + jnp.asarray(zero, part.dtype), x, identity
    )


def entering_2(x, axes, combine, identity):
    before = start = neutral_like(x, identity)
    so_far = x
    for axis in reversed(axes):
        peers, index = (lax.axis_size(axis), lax.axis_index(axis))
        pieces = jax.tree.map(lambda part: lax.all_gather(part, axis), so_far)
        inside, so_far = (start, start)
        for k in range(peers):
            passed = k < index
            so_far = combine(so_far, jax.tree.map(lambda part: part[k], pieces))
            inside = jax.tree.map(lambda new, old: jnp.where(passed, new, old), so_far, inside)
        before = combine(inside, before)
    return before


def prefix_by_axis(x, axes, combine, identity):
    before = start = neutral_like(x, identity)
    so_far = x
    for axis in reversed(axes):
        peers, index = (lax.axis_size(axis), lax.axis_index(axis))
        pieces = jax.tree.map(
            lambda part, kind: lax.all_gather(part.astype(kind), axis),
            so_far,
            (jnp.bfloat16, jnp.bfloat16),
        )
        inside, so_far = (start, start)
        for k in reversed(range(peers)):
            passed = k > index
            so_far = combine(
                so_far, jax.tree.map(lambda part, own: part[k].astype(own.dtype), pieces, x)
            )
            inside = jax.tree.map(lambda new, old: jnp.where(passed, new, old), so_far, inside)
        before = combine(inside, before)
    return before


def from_everyone(x, axis):
    peers = lax.axis_size(axis)
    return lax.all_to_all(jnp.broadcast_to(x[None], (peers, *x.shape)), axis, 0, 0, tiled=True)


def of_everyone(x, axis):
    return from_everyone(x, axis).sum(axis=0)


def cut_along(x, dim, peers):
    lengths = x.shape
    parts = x.reshape(*lengths[:dim], peers, lengths[dim] // peers, *lengths[dim + 1 :])
    return jnp.moveaxis(parts, dim, 0)


def sum_at_owner(x, axis, dim):
    parts = cut_along(x, dim, lax.axis_size(axis))
    arrived = lax.all_to_all(parts, axis, split_axis=0, concat_axis=0, tiled=True)
    return arrived.astype(jnp.float32).sum(axis=0)


def laid_out(parts, dim):
    parts = jnp.moveaxis(parts, 0, dim)
    lengths = parts.shape
    return parts.reshape(*lengths[:dim], lengths[dim] * lengths[dim + 1], *lengths[dim + 2 :])


def collect(x, axis, dim):
    return laid_out(from_everyone(x, axis), dim)


def block_terms(keys, queries, logs, scal, starts, forward):
    seg = jnp.cumsum(starts)
    cum = jnp.cumsum(logs, axis=0)
    excl = cum - logs
    scores = jnp.dot(queries, keys.T, preferred_element_type=jnp.float32)
    length = keys.shape[0]
    rows_idx = lax.broadcasted_iota(jnp.int32, (length, length), 0)
    cols_idx = lax.broadcasted_iota(jnp.int32, (length, length), 1)
    same = seg[:, None] == seg[None, :]
    cumt = cum.T
    exct = excl.T
    if forward:
        inside = same & (cols_idx <= rows_idx)
        expo = cumt[:, :, None] - cumt[:, None, :]
    else:
        inside = same & (cols_idx >= rows_idx)
        expo = exct[:, None, :] - exct[:, :, None]
    factor = jnp.exp(jnp.where(inside[None], expo, -jnp.inf))
    weights = (factor * scores[None] * scal.T[:, None, :]).astype(jnp.bfloat16)
    final = seg[-1]
    top = cum[-1]
    if forward:
        state_w = jnp.exp(jnp.where((seg == final)[:, None], top[None, :] - cum, -jnp.inf))
        carry_w = jnp.exp(jnp.where((seg == 0)[:, None], cum, -jnp.inf))
    else:
        state_w = jnp.exp(jnp.where((seg == 0)[:, None], excl, -jnp.inf))
        carry_w = jnp.exp(jnp.where((seg == final)[:, None], top[None, :] - excl, -jnp.inf))
    keyed = ((state_w * scal).T[:, :, None] * keys.astype(jnp.float32)[None]).astype(jnp.bfloat16)
    passing = jnp.where(final == 0, jnp.exp(top), jnp.zeros_like(top))
    return (weights, keyed, passing, carry_w)


def compose(earlier, later):
    return (later[0] * earlier[0], later[0][:, None, None] * earlier[1] + later[1])


def local_terms(acts3, keys, queries, logs, scal, starts, forward):
    weights, keyed, passing, carry_w = block_terms(keys, queries, logs, scal, starts, forward)
    inner = jnp.einsum("gij,jgp->igp", weights, acts3, preferred_element_type=jnp.float32)
    local = jnp.einsum("gjn,jgp->gnp", keyed, acts3, preferred_element_type=jnp.float32)
    return (inner, local, passing, carry_w)


def entering_terms(queries, state, carry_w):
    entering = jnp.einsum(
        "in,gnp->igp", queries.astype(jnp.float32), state, precision=lax.Precision.HIGHEST
    )
    return carry_w[:, :, None] * entering


def pool_rows(values):
    count = values.shape[0] // POOL
    return jnp.sum(values.reshape(count, POOL, values.shape[1]), axis=1) * (1.0 / POOL)


def split_project(rows, weight):
    upper = rows.astype(jnp.bfloat16)
    lower = (rows - upper.astype(jnp.float32)).astype(jnp.bfloat16)
    first = jnp.dot(upper, weight, preferred_element_type=jnp.float32)
    return first + jnp.dot(lower, weight, preferred_element_type=jnp.float32)


def body(
    inner_acts,
    gate_input,
    forward_keys,
    forward_queries,
    backward_keys,
    backward_queries,
    decay_codes,
    clip_start,
    skip_gain,
    norm_gain,
    out_weight,
):
    length = inner_acts.shape[0]
    heads_local = skip_gain.shape[0]
    head_size = inner_acts.shape[1] // heads_local
    total_tokens = lax.axis_size(SEQ) * length
    rate = decay_codes.astype(jnp.float32) / (32.0 * total_tokens)
    rate = jnp.repeat(rate, SPAN, axis=1)
    logs = jnp.log1p(-rate)
    scal = jnp.sqrt(rate * (2.0 - rate))
    acts3 = inner_acts.reshape(length, heads_local, head_size)
    inner_f, local_f, pass_f, carry_f = local_terms(
        acts3, forward_keys, forward_queries, logs[0], scal[0], clip_start, True
    )
    inner_b, local_b, pass_b, carry_b = local_terms(
        acts3, backward_keys, backward_queries, logs[1], scal[1], clip_start, False
    )
    identity = (jnp.ones_like(pass_f), jnp.zeros_like(local_f))
    state_f = entering_2((pass_f, local_f), SEQ, compose, identity)[1]
    state_b = prefix_by_axis((pass_b, local_b), SEQ, compose, identity)[1]
    ahead = inner_f + entering_terms(forward_queries, state_f, carry_f)
    behind = inner_b + entering_terms(backward_queries, state_b, carry_b)
    total = ahead + behind + skip_gain[None, :, None] * acts3.astype(jnp.float32)
    gated = total.reshape(length, heads_local * head_size) * jax.nn.silu(
        gate_input.astype(jnp.float32)
    )
    squares = of_everyone(jnp.sum(gated * gated, axis=1), "chan")
    meansq = squares / E
    hidden = (gated * lax.rsqrt(meansq + 1e-05)[:, None] * norm_gain[None, :]).astype(jnp.bfloat16)
    pooled = pool_rows(hidden.astype(jnp.float32))
    summed = sum_at_owner(split_project(pooled, out_weight).astype(jnp.bfloat16), "chan", 0)
    mixed = collect(summed.astype(jnp.bfloat16), "chan", 0)
    return mixed


def solution(mesh):
    torus = Mesh(
        mesh.devices.reshape(8, 4, 2, mesh.shape["chan"]), ("seq_0", "seq_1", "seq_2", "chan")
    )
    return jax.shard_map(
        body,
        mesh=torus,
        in_specs=(
            P(SEQ, "chan"),
            P(SEQ, "chan"),
            P(SEQ, None),
            P(SEQ, None),
            P(SEQ, None),
            P(SEQ, None),
            P(None, SEQ, "chan"),
            P(SEQ),
            P("chan"),
            P("chan"),
            P("chan", None),
        ),
        out_specs=P(SEQ, None),
        check_vma=False,
    )
```

profile of v0, /device:TPU:6, one launch (start us, length us, event | category | flops | bytes accessed | tf_op | source)
XLA Modules:
  0.0 222.3 jit_solution(9570610254621518333)
XLA Ops:
  6.5 1.1 reduce-window.21
  8.0 0.6 slice.215
  9.2 0.7 broadcast_compare_fusion
  9.9 1.3 copy.34
  11.2 0.8 convert_multiply_fusion.1
  12.2 1.1 reduce-window.29
  13.5 1.1 reduce-window.25
  14.8 0.9 convert_element_type.354
  15.8 0.7 select_exponential_fusion.1
  16.8 0.8 fusion.17
  17.5 2.2 all-gather
  19.7 1.8 all-gather.2
  21.5 11.6 %all-gather.3 = f32[4,1,8]{2,1,0:T(1,128)S(1)} all-gather(f32[1,1,8]{2,1,0:T(1,128)S(1)} %get-tuple-element.53), channel_id=1, replica_groups=mesh['seq_0'=8,'seq_1'=4,'seq_2'=2,'chan'=8] {'seq_1'}, dimensions={0}, use_global_device_ids=true | all-gather | bytes 160 | tf_op jit(solution)/shard_map/all_gather | solution.py:24
  33.1 0.6 fusion.203
  33.7 0.8 bitcast_add_fusion.4
  34.8 1.8 all-gather.5
  36.6 7.0 %all-gather.6 = bf16[4,1,8]{2,1,0:T(2,128)(2,1)S(1)} all-gather(bf16[1,1,8]{2,1,0:T(2,128)(2,1)S(1)} %multiply_convert_fusion.15), channel_id=1, replica_groups=mesh['seq_0'=8,'seq_1'=4,'seq_2'=2,'chan'=8] {'seq_1'}, dimensions={0}, use_global_device_ids=true | all-gather | bytes 80 | tf_op jit(solution)/shard_map/all_gather | solution.py:40
  43.6 0.8 convolution_convert_fusion
  44.4 2.0 all-gather.1
  47.6 15.9 %all_gather.64 = bf16[4,8,128,64]{2,3,1,0:T(8,128)(2,1)S(1)} all-gather(bf16[1,8,128,64]{2,3,1,0:T(8,128)(2,1)S(1)} %fusion.50), channel_id=1, replica_groups=mesh['seq_0'=8,'seq_1'=4,'seq_2'=2,'chan'=8] {'seq_1'}, dimensions={0}, use_global_device_ids=true | all-gather | bytes 655360 | tf_op jit(solution)/shard_map/all_gather | solution.py:40
  64.2 0.9 fusion.44
  65.1 1.3 multiply_multiply_fusion
  66.4 2.0 multiply_add_fusion
  68.5 1.3 fusion.216
  69.7 18.9 %all-gather.7 = bf16[8,1,8]{2,1,0:T(2,128)(2,1)S(1)} all-gather(bf16[1,1,8]{2,1,0:T(2,128)(2,1)} %fusion.216), channel_id=1, replica_groups=mesh['seq_0'=8,'seq_1'=4,'seq_2'=2,'chan'=8] {'seq_0'}, dimensions={0}, use_global_device_ids=true | all-gather | bytes 144 | tf_op jit(solution)/shard_map/all_gather | solution.py:40
  88.6 13.6 %all-gather.4 = f32[8,1,8]{2,1,0:T(1,128)S(1)} all-gather(f32[1,1,8]{2,1,0:T(1,128)} %get-tuple-element.41), channel_id=1, replica_groups=mesh['seq_0'=8,'seq_1'=4,'seq_2'=2,'chan'=8] {'seq_0'}, dimensions={0}, use_global_device_ids=true | all-gather | bytes 288 | tf_op jit(solution)/shard_map/all_gather | solution.py:24
  102.2 0.9 slice_reduce_fusion.2
  103.6 0.6 fusion.213
  104.2 0.6 slice_bitcast_fusion.41
  104.8 0.7 add_bitcast_fusion.2
  105.5 0.7 slice_bitcast_fusion.27
  106.3 1.4 select_exponential_fusion
  107.7 1.1 compare_and_fusion.1
  108.8 1.2 fusion.229
  110.3 3.6 %fusion.5 = f32[512,8,64]{0,2,1:T(8,128)} fusion(bf16[512,8,64]{0,2,1:T(8,128)(2,1)S(1)} %bitcast.442, f32[8,512]{1,0:T(8,128)S(1)} %get-tuple-element.23, f32[512,512]{1,0:T(8,128)S(1)} %fusion.229, f32[8,512]{1,0:T(8,128)S(1)} %get-tuple-element.18, pred[512,512]{1,0:T(8,128)(4,1)S(1)} %get-tuple-element.47), kind=kOutput, calls=%fused_computation.12 | convolution fusion | flops 278921216 | bytes 2916352 | tf_op jit(solution)/shard_map/gij,jgp->igp/dot_general | solution.py:124
  113.9 3.6 %fusion.6 = f32[512,8,64]{0,2,1:T(8,128)} fusion(bf16[512,8,64]{0,2,1:T(8,128)(2,1)S(1)} %bitcast.443, f32[8,512]{1,0:T(8,128)S(1)} %get-tuple-element.22, f32[512,512]{1,0:T(8,128)S(1)} %fusion.228, f32[8,512]{1,0:T(8,128)S(1)} %add_bitcast_fusion.2, pred[512,512]{1,0:T(8,128)(4,1)S(1)} %get-tuple-element.46), kind=kOutput, calls=%fused_computation.13 | convolution fusion | flops 278921216 | bytes 2916352 | tf_op jit(solution)/shard_map/gij,jgp->igp/dot_general | solution.py:124
  117.5 3.8 %fusion.12 = f32[512,8,64]{0,2,1:T(8,128)} fusion(f32[512,8,64]{0,2,1:T(8,128)} %fusion.5, f32[512,8]{0,1:T(8,128)} %get-tuple-element.17, bf16[8,8,128,64]{2,3,1,0:T(8,128)(2,1)} %all-gather.16.cloned.1.call-done, bf16[512,128]{1,0:T(8,128)(2,1)S(1)} %copy-done.7, f32[8]{0:T(128)} %copy-done.19, f32[8]{0:T(128)} %copy-done.24, f32[8]{0:T(128)} %copy-done.18, ...), kind=kOutput, calls=%fused_computation.19 | convolution fusion | flops 406913024 | bytes 4080142 | tf_op jit(solution)/shard_map/in,gnp->igp/dot_general | solution.py:130
  121.2 34.4 %all-gather.14.cloned.1.call-done = f32[8,8,128,64]{2,3,1,0:T(8,128)} async-done(((f32[1,8,128,64]{2,3,1,0:T(8,128)}), f32[8,8,128,64]{2,3,1,0:T(8,128)}) %all-gather.14.cloned.1.call-update) | async-done | bytes 2097168 | tf_op jit(solution)/shard_map/all_gather | solution.py:24
  155.7 4.9 %fusion.10 = f32[512,8,64]{0,2,1:T(8,128)} fusion(f32[512,8,64]{0,2,1:T(8,128)} %fusion.12, f32[512,8,64]{0,2,1:T(8,128)} %fusion.6, bf16[512,8,64]{0,2,1:T(8,128)(2,1)} %bitcast.441, f32[8]{0:T(128)} %param.19, f32[512,8]{0,1:T(8,128)S(1)} %copy-done.14, f32[8,8,128,64]{2,3,1,0:T(8,128)} %all-gather.14.cloned.1.call-done, ...), kind=kOutput, calls=%fused_computation.17 | convolution fusion | flops 407044096 | bytes 7488046 | tf_op jit(solution)/shard_map/in,gnp->igp/dot_general | solution.py:130
  160.5 1.6 copy.35
  162.1 1.5 multiply_reduce_fusion
  163.6 14.3 %all_to_all.16 = f32[8,1,512]{2,1,0:T(1,128)S(1)} all-to-all(f32[8,1,512]{2,1,0:T(1,128)S(1)} %broadcast_in_dim.63), channel_id=1, replica_groups=mesh['seq_0'=8,'seq_1'=4,'seq_2'=2,'chan'=8] {'chan'}, dimensions={0} | all-to-all | bytes 32768 | tf_op jit(solution)/shard_map/all_to_all | solution.py:57
  178.0 2.4 %fusion.22 = f32[512,512]{1,0:T(8,128)} fusion(f32[512]{0:T(512)S(1)} %copy-done.16, f32[512]{0:T(512)S(1)} %add_rsqrt_fusion, f32[512,512]{1,0:T(8,128)S(1)} %copy.35, bf16[512,512]{1,0:T(8,128)(2,1)} %param.12), kind=kLoop, calls=%fused_computation.38 | loop fusion | flops 2621440 | bytes 2625536 | tf_op jit(solution)/shard_map/reshape | solution.py:138
  180.4 1.5 reshape.477
  181.9 0.6 reduce_sum.41
  183.4 15.7 %all_to_all.17 = bf16[8,16,2048]{2,1,0:T(8,128)(2,1)S(1)} all-to-all(bf16[8,16,2048]{2,1,0:T(8,128)(2,1)S(1)} %bitcast.436), channel_id=1, replica_groups=mesh['seq_0'=8,'seq_1'=4,'seq_2'=2,'chan'=8] {'chan'}, dimensions={0} | all-to-all | bytes 1048576 | tf_op jit(solution)/shard_map/all_to_all | solution.py:72
  199.3 15.7 %all_to_all.18 = bf16[8,16,2048]{2,1,0:T(8,128)(2,1)S(1)} all-to-all(bf16[8,16,2048]{2,1,0:T(8,128)(2,1)S(1)} %broadcast_in_dim.64), channel_id=1, replica_groups=mesh['seq_0'=8,'seq_1'=4,'seq_2'=2,'chan'=8] {'chan'}, dimensions={0} | all-to-all | bytes 1048576 | tf_op jit(solution)/shard_map/all_to_all | solution.py:57
  215.0 0.8 copy.39
  (90 shorter events, 5.1 us)
Async XLA Ops:
  6.5 176.0 %copy-start = (bf16[512,2048]{1,0:T(8,128)(2,1)S(1)}, bf16[512,2048]{1,0:T(8,128)(2,1)}, u32[]{:S(2)}) copy-start(bf16[512,2048]{1,0:T(8,128)(2,1)} %param.21) | copy-start | bytes 6291460
  6.5 59.9 %all-gather.12.cloned.1.call-start = ((), (), s32[]{:S(2)}) async-start(), calls=%async_computation.3 | async-start | bytes 1310720 | tf_op jit(solution)/shard_map/all_gather | solution.py:24
  8.0 8.8 %copy-start.10 = (s32[512]{0:T(512)}, s32[512]{0:T(512)S(1)}, u32[]{:S(2)}) copy-start(s32[512]{0:T(512)S(1)} %get-tuple-element.16) | copy-start | bytes 6148
  9.9 24.6 %copy-start.15 = (pred[512]{0:T(512)(128)(4,1)}, pred[512]{0:T(512)(128)(4,1)S(1)}, u32[]{:S(2)}) copy-start(pred[512]{0:T(512)(128)(4,1)S(1)} %broadcast_compare_fusion) | copy-start | bytes 1540
  11.2 32.5 %copy-start.3 = (bf16[512,512]{0,1:T(8,128)(2,1)}, bf16[512,512]{0,1:T(8,128)(2,1)S(1)}, u32[]{:S(2)}) copy-start(bf16[512,512]{0,1:T(8,128)(2,1)S(1)} %copy.34) | copy-start | bytes 1572868
  11.2 32.4 %copy-start.1 = (bf16[512,128]{1,0:T(8,128)(2,1)S(1)}, bf16[512,128]{1,0:T(8,128)(2,1)}, u32[]{:S(2)}) copy-start(bf16[512,128]{1,0:T(8,128)(2,1)} %param.15) | copy-start | bytes 393220
  12.1 31.5 %copy-start.5 = (f32[2,512,8]{1,2,0:T(8,128)}, f32[2,512,8]{1,2,0:T(8,128)S(1)}, u32[]{:S(2)}) copy-start(f32[2,512,8]{1,2,0:T(8,128)S(1)} %get-tuple-element.24) | copy-start | bytes 98308
  12.1 31.5 %copy-start.6 = (f32[2,512,8]{1,2,0:T(8,128)}, f32[2,512,8]{1,2,0:T(8,128)S(1)}, u32[]{:S(2)}) copy-start(f32[2,512,8]{1,2,0:T(8,128)S(1)} %get-tuple-element.25) | copy-start | bytes 98308
  14.8 1.8 copy-start.12
  16.7 26.9 %copy-start.9 = (f32[512,8]{0,1:T(8,128)}, f32[512,8]{0,1:T(8,128)S(1)}, u32[]{:S(2)}) copy-start(f32[512,8]{0,1:T(8,128)S(1)} %get-tuple-element.14) | copy-start | bytes 49156
  21.5 22.1 %copy-start.20 = (f32[8]{0:T(128)}, f32[8]{0:T(128)S(1)}, u32[]{:S(2)}) copy-start(f32[8]{0:T(128)S(1)} %get-tuple-element.54) | copy-start | bytes 100
  33.1 10.5 %copy-start.13 = (f32[4,1,8]{2,1,0:T(1,128)}, f32[4,1,8]{2,1,0:T(1,128)S(1)}, u32[]{:S(2)}) copy-start(f32[4,1,8]{2,1,0:T(1,128)S(1)} %all-gather.3) | copy-start | bytes 388
  33.7 13.3 %copy-start.17 = (f32[8]{0:T(128)}, f32[8]{0:T(128)S(1)}, u32[]{:S(2)}) copy-start(f32[8]{0:T(128)S(1)} %get-tuple-element.52) | copy-start | bytes 100
  34.5 82.9 %all-gather.16.cloned.1.call-start = ((), (), s32[]{:S(2)}) async-start(), calls=%async_computation.5 | async-start | bytes 1179648 | tf_op jit(solution)/shard_map/all_gather | solution.py:40
  43.5 20.0 %copy-start.11 = (bf16[4,1,8]{2,1,0:T(2,128)(2,1)}, bf16[4,1,8]{2,1,0:T(2,128)(2,1)S(1)}, u32[]{:S(2)}) copy-start(bf16[4,1,8]{2,1,0:T(2,128)(2,1)S(1)} %all-gather.6) | copy-start | bytes 196
  46.4 0.6 copy-start.24
  47.0 0.5 copy-start.19
  47.0 16.6 %copy-start.18 = (f32[8]{0:T(128)}, f32[8]{0:T(128)S(1)}, u32[]{:S(2)}) copy-start(f32[8]{0:T(128)S(1)} %get-tuple-element.48) | copy-start | bytes 100
  63.6 0.5 copy-start.21
  63.6 0.6 copy-start.22
  63.6 0.6 copy-start.23
  65.1 90.6 %all-gather.14.cloned.1.call-start = ((), (), s32[]{:S(2)}) async-start(), calls=%async_computation.4 | async-start | bytes 2359296 | tf_op jit(solution)/shard_map/all_gather | solution.py:24
  69.7 40.3 %copy-start.2 = (bf16[512,128]{1,0:T(8,128)(2,1)S(1)}, bf16[512,128]{1,0:T(8,128)(2,1)}, u32[]{:S(2)}) copy-start(bf16[512,128]{1,0:T(8,128)(2,1)} %param.13) | copy-start | bytes 393220
  69.7 40.3 %copy-start.8 = (bf16[512,128]{1,0:T(8,128)(2,1)S(1)}, bf16[512,128]{1,0:T(8,128)(2,1)}, u32[]{:S(2)}) copy-start(bf16[512,128]{1,0:T(8,128)(2,1)} %param.14) | copy-start | bytes 393220
  69.7 40.6 %copy-start.4 = (bf16[512,512]{0,1:T(8,128)(2,1)S(1)}, bf16[512,512]{0,1:T(8,128)(2,1)}, u32[]{:S(2)}) copy-start(bf16[512,512]{0,1:T(8,128)(2,1)} %copy-done.3) | copy-start | bytes 1572868
  113.9 3.6 %copy-start.7 = (bf16[512,128]{1,0:T(8,128)(2,1)S(1)}, bf16[512,128]{1,0:T(8,128)(2,1)}, u32[]{:S(2)}) copy-start(bf16[512,128]{1,0:T(8,128)(2,1)} %param.16) | copy-start | bytes 393220
  117.5 38.2 %copy-start.14 = (f32[512,8]{0,1:T(8,128)S(1)}, f32[512,8]{0,1:T(8,128)}, u32[]{:S(2)}) copy-start(f32[512,8]{0,1:T(8,128)} %get-tuple-element.9) | copy-start | bytes 49156
  160.5 17.4 %copy-start.16 = (f32[512]{0:T(512)S(1)}, f32[512]{0:T(512)}, u32[]{:S(2)}) copy-start(f32[512]{0:T(512)} %param.20) | copy-start | bytes 6148
Sparse Core Ops, SparseCore 0:
  34.6 31.6 all-gather.11
  68.4 43.0 all-gather.15
  113.6 42.0 all-gather.13
where the time goes:
time: 223 us; the launch traced here: 222 us
  blocking collectives  120 us (54%)
  waiting for transfers between devices  34.5 us (15%)
  other arithmetic  24.3 us (11%)
  matrix products  19.8 us (9%)
  between operations  14.1 us (6%)
  local copies, waits for them, and re-layouts  9.09 us (4%)
    all_gather x5, blocking collectives, prefix_by_axis(): lax.all_gather(part.astype(kind), axis)  45.6 us
    all_gather x2, waiting for transfers between devices, entering_2(): pieces = jax.tree.map(lambda part: lax.all_gather(part, axis), so_far)  34.4 us
    all_to_all x2, blocking collectives, from_everyone(): lax.all_to_all(jnp.broadcast_to(x[None], (peers, *x.shape)), axis, 0, 0,...  30 us
    all_gather x4, blocking collectives, entering_2(): pieces = jax.tree.map(lambda part: lax.all_gather(part, axis), so_far)  29.2 us
    all_to_all x1, blocking collectives, sum_at_owner(): lax.all_to_all(parts, axis, split_axis=0, concat_axis=0, tiled=True)  15.7 us
    dot_general x2, matrix products, entering_terms(): jnp.einsum('in,gnp->igp', queries.astype(jnp.float32), state, precision=l...  8.63 us
    dot_general x2, matrix products, local_terms(): jnp.einsum('gij,jgp->igp', weights, acts3, preferred_element_type=jnp.flo...  7.15 us
  transfers between devices with their start and end apart: 3, of which 1 were waited for; matrix products, arithmetic and copies ran while one was open for 12% of the time, Pallas kernels for 0%

commit v1 on v0

v1 whole, which is shorter than its diff:
```python
import functools

import jax
import jax.numpy as jnp
from jax import lax
from jax.experimental import pallas as pl
from jax.experimental.pallas import tpu as pltpu
from jax.sharding import Mesh
from jax.sharding import PartitionSpec as P

SPAN = 256
POOL = 4
CH = 128
HEAD = 64
LANES = 128
SEQ = ("seq_0", "seq_1", "seq_2")
MESH = pl.DeviceIdType.MESH
F32 = jnp.float32
BF = jnp.bfloat16


def log_keep(rate):
    acc = jnp.full_like(rate, 1.0 / 12)
    for n in range(11, 0, -1):
        acc = acc * rate + 1.0 / n
    return -rate * acc


def dot_t(a, b):
    return lax.dot_general(a, b, (((0,), (0,)), ((), ())), preferred_element_type=F32)


def dot_nt(a, b):
    return lax.dot_general(a, b, (((1,), (1,)), ((), ())), preferred_element_type=F32)


def dot(a, b):
    return jnp.dot(a, b, preferred_element_type=F32)


def chains(n_y):
    far, near = n_y // 2, n_y // 2 - 1
    return ((1, 0, far), (-1, 1, far), (-1, 0, near), (1, 1, near))


def layer_kernel(
    sizes,
    codes_ref,
    skip_ref,
    clip_ref,
    gain_ref,
    acts_hbm,
    gate_hbm,
    fk_hbm,
    fq_hbm,
    bk_hbm,
    bq_hbm,
    w_hbm,
    out_hbm,
    x_ref,
    z_ref,
    fk_ref,
    fq_ref,
    bk_ref,
    bq_ref,
    w_ref,
    y_scr,
    silu_scr,
    st_scr,
    carry_scr,
    cw_scr,
    sbuf,
    recv1,
    pbuf,
    recvp,
    a_scr,
    q_scr,
    zbuf,
    recvz,
    zpbuf,
    recvzp,
    ebuf,
    recv3,
    qbuf,
    recvq,
    part,
    rs_send,
    rs_recv,
    obuf,
    in_sem,
    p1s,
    p1r,
    pps,
    ppr,
    zs,
    zr,
    zps,
    zpr,
    p3s,
    p3r,
    sqs,
    sqr,
    rss,
    rsr,
    ags,
    agr,
    out_sem,
):
    n_z, n_x, n_c, n_y = sizes
    n_p = n_x * n_c
    tokens, width = x_ref.shape
    n_ch = tokens // CH
    n_sp = tokens // SPAN
    heads = width // HEAD
    tiles = width // LANES
    states = fk_ref.shape[1]
    prow = states // n_p
    total_tokens = n_z * n_x * n_c * tokens
    dim = w_ref.shape[1]
    half = dim // 2
    rows_out = tokens // POOL
    orow = rows_out // n_y

    iz = lax.axis_index("seq_0")
    ix = lax.axis_index("seq_1")
    ic = lax.axis_index("seq_2")
    iy = lax.axis_index("chan")
    me = ix * n_c + ic

    def plane_peer(k, sign=1):
        px = lax.rem(ix + sign * (k // n_c) + n_x, n_x)
        pc = lax.rem(ic + sign * (k % n_c) + n_c, n_c)
        return px, pc, px * n_c + pc

    def z_peer(k, sign=1):
        return lax.rem(iz + sign * k + n_z, n_z)

    def y_peer(k, sign=1):
        return lax.rem(iy + sign * k + 2 * n_y, n_y)

    barrier = pltpu.get_barrier_semaphore()
    for k in range(1, n_p):
        px, pc, _ = plane_peer(k)
        pl.semaphore_signal(
            barrier, inc=1, device_id={"seq_1": px, "seq_2": pc}, device_id_type=MESH
        )
    for k in range(1, n_z):
        pl.semaphore_signal(barrier, inc=1, device_id={"seq_0": z_peer(k)}, device_id_type=MESH)
    for k in range(1, n_y):
        pl.semaphore_signal(barrier, inc=1, device_id={"chan": y_peer(k)}, device_id_type=MESH)

    loads = [
        pltpu.make_async_copy(src, dst, in_sem.at[n])
        for n, (src, dst) in enumerate(
            (
                (acts_hbm, x_ref),
                (fk_hbm, fk_ref),
                (bk_hbm, bk_ref),
                (fq_hbm, fq_ref),
                (bq_hbm, bq_ref),
                (gate_hbm, z_ref),
                (w_hbm, w_ref),
            )
        )
    ]
    for load in loads:
        load.start()

    low = lax.broadcasted_iota(jnp.int32, (1, LANES), 1) < HEAD
    logs, scal = [], []
    for d in range(2):
        logs.append([])
        scal.append([])
        for s in range(n_sp):
            rates = [
                jnp.full((1, LANES), codes_ref[d, s, h].astype(F32)) * (1.0 / (32.0 * total_tokens))
                for h in range(heads)
            ]
            logs[d].append([log_keep(r) for r in rates])
            scal[d].append([jnp.sqrt(r * (2.0 - r)) for r in rates])

    def as_row(items):
        return jnp.concatenate(
            [jnp.where(low, items[2 * t], items[2 * t + 1]) for t in range(tiles)], axis=1
        )

    log_row = [[as_row(logs[d][s]) for s in range(n_sp)] for d in range(2)]
    scal_row = [[as_row(scal[d][s]) for s in range(n_sp)] for d in range(2)]

    rows = lax.broadcasted_iota(jnp.int32, (CH, CH), 0)
    cols = lax.broadcasted_iota(jnp.int32, (CH, CH), 1)
    lower = rows >= cols
    upper = rows <= cols
    starts = clip_ref[...].astype(F32).astype(BF)
    seg_row = dot(starts, upper.astype(F32).astype(BF))
    seg_col = dot_nt(lower.astype(F32).astype(BF), starts)
    seg_c = [seg_col[:, a : a + 1] for a in range(n_ch)]
    fin = [seg_row[a : a + 1, CH - 1 : CH] for a in range(n_ch)]
    first_m = [(seg_c[a] == 0.0).astype(F32) for a in range(n_ch)]
    last_m = [(seg_c[a] == fin[a]).astype(F32) for a in range(n_ch)]
    clear = [(fin[a] == 0.0).astype(F32) for a in range(n_ch)]
    passing = [
        [jnp.exp(float(CH) * log_row[d][a * CH // SPAN]) * clear[a] for a in range(n_ch)]
        for d in range(2)
    ]

    step_f = lax.broadcasted_iota(jnp.int32, (CH, width), 0).astype(F32)
    grow = (
        [jnp.exp(log_row[0][s] * (CH - 1.0 - step_f)) * scal_row[0][s] for s in range(n_sp)],
        [jnp.exp(log_row[1][s] * step_f) * scal_row[1][s] for s in range(n_sp)],
    )
    for n in range(3):
        loads[n].wait()

    def chunk(a):
        return pl.ds(a * CH, CH)

    total_pass = []
    for d in range(2):
        keys_ref = (fk_ref, bk_ref)[d]
        mask = (last_m, first_m)[d]
        order = range(n_ch) if d == 0 else range(n_ch - 1, -1, -1)
        state, through = None, None
        for a in order:
            if state is None:
                st_scr[d, a] = jnp.zeros((states, width), F32)
                carry_scr[d, a] = jnp.ones((8, width), F32)
            else:
                st_scr[d, a] = state
                carry_scr[d, a] = jnp.broadcast_to(through, (8, width))
            scaled = (x_ref[chunk(a), :].astype(F32) * (grow[d][a * CH // SPAN] * mask[a])).astype(BF)
            local = dot_t(keys_ref[chunk(a), :], scaled)
            state = local if state is None else passing[d][a] * state + local
            through = passing[d][a] if through is None else passing[d][a] * through
        for j in range(n_p):
            sbuf[j, d] = state[j * prow : (j + 1) * prow, :].astype(BF)
        for t in range(tiles):
            pbuf[d * tiles + t : d * tiles + t + 1, :] = through[:, t * LANES : (t + 1) * LANES]

    pl.semaphore_wait(barrier, (n_p - 1) + (n_z - 1) + (n_y - 1))

    def p1_copies(k):
        px, pc, pj = plane_peer(k)
        where = {"seq_1": px, "seq_2": pc}
        return (
            pltpu.make_async_remote_copy(
                pbuf, recvp.at[me], pps.at[k], ppr.at[k], device_id=where, device_id_type=MESH
            ),
            pltpu.make_async_remote_copy(
                sbuf.at[pj], recv1.at[me], p1s.at[k], p1r.at[k], device_id=where, device_id_type=MESH
            ),
        )

    def p1_arrivals(k):
        px, pc, pj = plane_peer(k, -1)
        where = {"seq_1": px, "seq_2": pc}
        return (
            pltpu.make_async_remote_copy(
                pbuf, recvp.at[pj], pps.at[k], ppr.at[k], device_id=where, device_id_type=MESH
            ),
            pltpu.make_async_remote_copy(
                sbuf.at[pj], recv1.at[pj], p1s.at[k], p1r.at[k], device_id=where, device_id_type=MESH
            ),
        )

    sent = []
    far_first = sorted(range(1, n_p), key=lambda k: -min(k // n_c, n_x - k // n_c))
    for k in far_first:
        for copy in p1_copies(k):
            copy.start()
            sent.append(copy)
    recv1[me] = sbuf[me]
    recvp[me] = pbuf[...]

    loads[3].wait()
    loads[4].wait()
    apart = jnp.abs(rows - cols).astype(F32)
    left_m = jnp.where(low, 1.0, 0.0).astype(BF)
    right_m = jnp.where(low, 0.0, 1.0).astype(BF)
    for s in range(n_sp):
        decay = [
            jnp.exp(apart * jnp.where(lower, logs[0][s][h], logs[1][s][h])) for h in range(heads)
        ]
        for a in range(s * SPAN // CH, (s + 1) * SPAN // CH):
            same = seg_c[a] == seg_row[a : a + 1, :]
            ahead = jnp.where(
                same & lower, dot_nt(fq_ref[chunk(a), :], fk_ref[chunk(a), :]), 0.0
            )
            behind = jnp.where(
                same & upper, dot_nt(bq_ref[chunk(a), :], bk_ref[chunk(a), :]), 0.0
            )
            for t in range(tiles):
                pair = jnp.concatenate(
                    [
                        (
                            decay[h] * (scal[0][s][h] * ahead + scal[1][s][h] * behind)
                        ).astype(BF)
                        for h in (2 * t, 2 * t + 1)
                    ],
                    axis=1,
                )
                lanes = pl.ds(t * LANES, LANES)
                xt = x_ref[chunk(a), lanes]
                both = jnp.concatenate([xt * left_m, xt * right_m], axis=0)
                skip = jnp.where(low, skip_ref[2 * t], skip_ref[2 * t + 1])
                y_scr[chunk(a), lanes] = dot(pair, both) + skip * xt.astype(F32)

    for k in range(1, n_p):
        for copy in p1_arrivals(k):
            copy.wait_recv()

    def pass_row(ref, d):
        return jnp.concatenate(
            [ref[d * tiles + t : d * tiles + t + 1, :] for t in range(tiles)], axis=1
        )

    for d in range(2):
        order = range(n_p) if d == 0 else range(n_p - 1, -1, -1)
        state = jnp.zeros((prow, width), F32)
        through = jnp.ones((1, width), F32)
        for q in order:
            a_scr[d, q] = state
            q_scr[d, q] = jnp.broadcast_to(through, (8, width))
            factor = pass_row(recvp.at[q], d)
            state = factor * state + recv1[q, d].astype(F32)
            through = factor * through
        zbuf[d] = state.astype(BF)
        for t in range(tiles):
            zpbuf[d * tiles + t : d * tiles + t + 1, :] = through[:, t * LANES : (t + 1) * LANES]

    def z_copies(k):
        pz = z_peer(k)
        where = {"seq_0": pz}
        d = jnp.where(pz > iz, 0, 1)
        return (
            pltpu.make_async_remote_copy(
                zpbuf, recvzp.at[iz], zps.at[k], zpr.at[k], device_id=where, device_id_type=MESH
            ),
            pltpu.make_async_remote_copy(
                zbuf.at[d], recvz.at[iz], zs.at[k], zr.at[k], device_id=where, device_id_type=MESH
            ),
        )

    def z_arrivals(k):
        pz = z_peer(k, -1)
        where = {"seq_0": pz}
        return (
            pltpu.make_async_remote_copy(
                zpbuf, recvzp.at[pz], zps.at[k], zpr.at[k], device_id=where, device_id_type=MESH
            ),
            pltpu.make_async_remote_copy(
                zbuf.at[0], recvz.at[pz], zs.at[k], zr.at[k], device_id=where, device_id_type=MESH
            ),
        )

    for k in sorted(range(1, n_z), key=lambda k: -min(k, n_z - k)):
        for copy in z_copies(k):
            copy.start()
            sent.append(copy)
    recvz[iz] = jnp.zeros((prow, width), BF)
    recvzp[iz] = zpbuf[...]

    loads[5].wait()
    for a in range(n_ch):
        v = z_ref[chunk(a), :].astype(F32)
        silu_scr[chunk(a), :] = v / (1.0 + jnp.exp(-v))
    for s in range(n_sp):
        cw_scr[0, s] = jnp.exp(log_row[0][s] * (step_f + 1.0))
        cw_scr[1, s] = jnp.exp(log_row[1][s] * (float(CH) - step_f))

    for k in range(1, n_z):
        for copy in z_arrivals(k):
            copy.wait_recv()

    for d in range(2):
        state = jnp.zeros((prow, width), F32)
        for q in range(n_z) if d == 0 else range(n_z - 1, -1, -1):
            new = pass_row(recvzp.at[q], d) * state + recvz[q].astype(F32)
            state = jnp.where(q < iz if d == 0 else q > iz, new, state)
        for q in range(n_p):
            ebuf[q, d] = (a_scr[d, q] + q_scr[d, q][0:1, :] * state).astype(BF)

    def p3_copy(k, sign=1):
        px, pc, pj = plane_peer(k, sign)
        return pltpu.make_async_remote_copy(
            ebuf.at[pj],
            recv3.at[me if sign == 1 else pj],
            p3s.at[k],
            p3r.at[k],
            device_id={"seq_1": px, "seq_2": pc},
            device_id_type=MESH,
        )

    for k in far_first:
        copy = p3_copy(k)
        copy.start()
        sent.append(copy)
    recv3[me] = ebuf[me]
    for k in range(1, n_p):
        p3_copy(k, -1).wait_recv()

    for a in range(n_ch):
        s = a * CH // SPAN
        for d in range(2):
            entering = jnp.concatenate([recv3[q, d] for q in range(n_p)], axis=0).astype(F32)
            state = st_scr[d, a] + carry_scr[d, a][0:1, :] * entering
            mask = (first_m, last_m)[d]
            queries = (fq_ref, bq_ref)[d][chunk(a), :]
            y_scr[chunk(a), :] += (cw_scr[d, s] * mask[a]) * dot(queries, state.astype(BF))
        gated = y_scr[chunk(a), :] * silu_scr[chunk(a), :]
        y_scr[chunk(a), :] = gated
        squares = gated * gated
        lanes_sum = squares[:, :LANES]
        for t in range(1, tiles):
            lanes_sum = lanes_sum + squares[:, t * LANES : (t + 1) * LANES]
        qbuf[a : a + 1, :] = jnp.sum(lanes_sum.T, axis=0, keepdims=True)

    def q_copy(k, sign=1):
        py = y_peer(k, sign)
        return pltpu.make_async_remote_copy(
            qbuf,
            recvq.at[iy if sign == 1 else py],
            sqs.at[k],
            sqr.at[k],
            device_id={"chan": py},
            device_id_type=MESH,
        )

    for k in sorted(range(1, n_y), key=lambda k: -min(k, n_y - k)):
        copy = q_copy(k)
        copy.start()
        sent.append(copy)
    recvq[iy] = qbuf[...]
    for k in range(1, n_y):
        q_copy(k, -1).wait_recv()
    squares = recvq[0]
    for k in range(1, n_y):
        squares = squares + recvq[k]
    inv = lax.rsqrt(squares / float(n_y * width) + 1e-05)

    pool = jnp.where(
        lax.broadcasted_iota(jnp.int32, (CH // POOL, CH), 0)
        == lax.broadcasted_iota(jnp.int32, (CH // POOL, CH), 1) // POOL,
        1.0 / POOL,
        0.0,
    ).astype(BF)
    gain = gain_ref[...]
    pooled = []
    for a in range(n_ch):
        inv_col = jnp.broadcast_to(inv[a : a + 1, :], (CH, LANES)).T
        inv_full = jnp.concatenate([inv_col] * tiles, axis=1)
        hidden = (y_scr[chunk(a), :] * inv_full * gain).astype(BF)
        pooled.append(dot(pool, hidden))
    pooled = jnp.concatenate(pooled, axis=0)
    high = pooled.astype(BF)
    rest = (pooled - high.astype(F32)).astype(BF)
    loads[6].wait()
    for c in range(2):
        cut = pl.ds(c * half, half)
        w = w_ref[:, cut]
        result = dot(high, w) + dot(rest, w)
        for p in range(n_y):
            part[p, :, cut] = result[p * orow : (p + 1) * orow, :]

    links = [c for c in enumerate(chains(n_y)) if c[1][2] > 0]

    def rs_copy(n, sign, s):
        return pltpu.make_async_remote_copy(
            rs_send.at[n, s],
            rs_recv.at[n, s],
            rss.at[n, s],
            rsr.at[n, s],
            device_id={"chan": y_peer(sign)},
            device_id_type=MESH,
        )

    for s in range(n_y // 2):
        for n, (sign, h, length) in links:
            if s >= length:
                continue
            cut = pl.ds(h * half, half)
            value = part[y_peer(sign * (length - s)), :, cut]
            if s > 0:
                rs_copy(n, sign, s - 1).wait_recv()
                value = value + rs_recv[n, s - 1].astype(F32)
            rs_send[n, s] = value.astype(BF)
            copy = rs_copy(n, sign, s)
            copy.start()
            sent.append(copy)

    def out_rows(p):
        return pl.ds(pl.multiple_of(p * orow, orow), orow)

    for h in range(2):
        cut = pl.ds(h * half, half)
        value = part[iy, :, cut]
        for n, (sign, hh, length) in links:
            if hh == h:
                rs_copy(n, sign, length - 1).wait_recv()
                value = value + rs_recv[n, length - 1].astype(F32)
        obuf[out_rows(iy), cut] = value.astype(BF)

    def ag_copy(n, sign, h, s, own):
        p = y_peer(-sign * s) if own else y_peer(-sign * (s + 1))
        view = obuf.at[out_rows(p), pl.ds(h * half, half)]
        return pltpu.make_async_remote_copy(
            view,
            view,
            ags.at[n, s],
            agr.at[n, s],
            device_id={"chan": y_peer(sign)},
            device_id_type=MESH,
        )

    for s in range(n_y // 2):
        for n, (sign, h, length) in links:
            if s >= length:
                continue
            if s > 0:
                ag_copy(n, sign, h, s - 1, False).wait_recv()
            copy = ag_copy(n, sign, h, s, True)
            copy.start()
            sent.append(copy)
    for n, (sign, h, length) in links:
        ag_copy(n, sign, h, length - 1, False).wait_recv()
    done = pltpu.make_async_copy(obuf, out_hbm, out_sem)
    done.start()
    for copy in sent:
        copy.wait_send()
    done.wait()


def body(
    inner_acts,
    gate_input,
    forward_keys,
    forward_queries,
    backward_keys,
    backward_queries,
    decay_codes,
    clip_start,
    skip_gain,
    norm_gain,
    out_weight,
):
    sizes = tuple(lax.axis_size(a) for a in SEQ) + (lax.axis_size("chan"),)
    n_z, n_x, n_c, n_y = sizes
    n_p = n_x * n_c
    tokens, width = inner_acts.shape
    states = forward_keys.shape[1]
    dim = out_weight.shape[1]
    n_ch, n_sp = tokens // CH, tokens // SPAN
    prow = states // n_p
    rows_out = tokens // POOL
    orow = rows_out // n_y
    steps = n_y // 2
    vmem = pltpu.VMEM
    dma = pltpu.SemaphoreType.DMA
    any_spec = pl.BlockSpec(memory_space=pl.ANY)
    smem_spec = pl.BlockSpec(memory_space=pltpu.SMEM)
    vmem_spec = pl.BlockSpec(memory_space=pltpu.VMEM)
    scratch = [
        vmem((tokens, width), BF),
        vmem((tokens, width), BF),
        vmem((tokens, states), BF),
        vmem((tokens, states), BF),
        vmem((tokens, states), BF),
        vmem((tokens, states), BF),
        vmem(out_weight.shape, BF),
        vmem((tokens, width), F32),
        vmem((tokens, width), F32),
        vmem((2, n_ch, states, width), F32),
        vmem((2, n_ch, 8, width), F32),
        vmem((2, n_sp, CH, width), F32),
        vmem((n_p, 2, prow, width), BF),
        vmem((n_p, 2, prow, width), BF),
        vmem((8, LANES), F32),
        vmem((n_p, 8, LANES), F32),
        vmem((2, n_p, prow, width), F32),
        vmem((2, n_p, 8, width), F32),
        vmem((2, prow, width), BF),
        vmem((n_z, prow, width), BF),
        vmem((8, LANES), F32),
        vmem((n_z, 8, LANES), F32),
        vmem((n_p, 2, prow, width), BF),
        vmem((n_p, 2, prow, width), BF),
        vmem((n_ch, LANES), F32),
        vmem((n_y, n_ch, LANES), F32),
        vmem((n_y, orow, dim), F32),
        vmem((4, steps, orow, dim // 2), BF),
        vmem((4, steps, orow, dim // 2), BF),
        vmem((rows_out, dim), BF),
        dma((7,)),
        dma((n_p,)),
        dma((n_p,)),
        dma((n_p,)),
        dma((n_p,)),
        dma((n_z,)),
        dma((n_z,)),
        dma((n_z,)),
        dma((n_z,)),
        dma((n_p,)),
        dma((n_p,)),
        dma((n_y,)),
        dma((n_y,)),
        dma((4, steps)),
        dma((4, steps)),
        dma((4, steps)),
        dma((4, steps)),
        dma,
    ]
    return pl.pallas_call(
        functools.partial(layer_kernel, sizes),
        out_shape=jax.ShapeDtypeStruct((rows_out, dim), BF),
        in_specs=[smem_spec, smem_spec, vmem_spec, vmem_spec] + [any_spec] * 7,
        out_specs=any_spec,
        scratch_shapes=scratch,
        compiler_params=pltpu.CompilerParams(
            collective_id=0, has_side_effects=True, vmem_limit_bytes=40 << 20
        ),
        name="layer",
    )(
        decay_codes,
        skip_gain,
        clip_start.reshape(n_ch, CH),
        norm_gain.reshape(1, width),
        inner_acts,
        gate_input,
        forward_keys,
        forward_queries,
        backward_keys,
        backward_queries,
        out_weight,
    )


def solution(mesh):
    torus = Mesh(
        mesh.devices.reshape(8, 4, 2, mesh.shape["chan"]), ("seq_0", "seq_1", "seq_2", "chan")
    )
    return jax.shard_map(
        body,
        mesh=torus,
        in_specs=(
            P(SEQ, "chan"),
            P(SEQ, "chan"),
            P(SEQ, None),
            P(SEQ, None),
            P(SEQ, None),
            P(SEQ, None),
            P(None, SEQ, "chan"),
            P(SEQ),
            P("chan"),
            P("chan"),
            P("chan", None),
        ),
        out_specs=P(SEQ, None),
        check_vma=False,
    )
```

time: 223 us -> 75.5 us (0.34)
  blocking collectives: 120 us -> 0 us
  Pallas kernels: 0 us -> 64 us
  waiting for transfers between devices: 34.5 us -> 0 us
  other arithmetic: 24.3 us -> 0 us
  matrix products: 19.8 us -> 0 us
  between operations: 14.1 us -> 0.02 us
    all_gather x9 -> x0, blocking collectives: 74.7 us -> none  [the longest x5 45.6 us: prefix_by_axis(): lax.all_gather(part.astype(kind), axis)]
    pallas_call x0 -> x1, Pallas kernels: none -> 64 us  [body(): pl.pallas_call(functools.partial(layer_kernel, sizes), out_shape=jax.Shap...]
    all_to_all x3 -> x0, blocking collectives: 45.7 us -> none  [the longest x2 30 us: from_everyone(): lax.all_to_all(jnp.broadcast_to(x[None], (peers, *x.shape)), axis, 0, 0,...]
    all_gather x3 -> x0, waiting for transfers between devices: 34.4 us -> none  [the longest x2 34.4 us: entering_2(): pieces = jax.tree.map(lambda part: lax.all_gather(part, axis), so_far)]
    dot_general x10 -> x0, matrix products: 19.8 us -> none  [the longest x2 8.63 us: entering_terms(): jnp.einsum('in,gnp->igp', queries.astype(jnp.float32), state, precision=l...]
    unnamed x52 -> x23, local copies, waits for them, and re-layouts: 3.16 us -> 10.8 us
    another operation x7 -> x0, other arithmetic: 4.24 us -> none
    mul x6 -> x0, other arithmetic: 3.58 us -> none  [the longest x4 2.46 us: compose(): later[0] * earlier[0]]
  transfers between devices with their start and end apart: 3 -> 0, of which waited for: 1 -> 0; matrix products, arithmetic and copies ran while one was open for 12% -> 0% of each run, Pallas kernels for 0% -> 0%
where the time goes in v1:
time: 75.5 us; the launch traced here: 74.8 us
  Pallas kernels  64 us (85%)
  local copies, waits for them, and re-layouts  10.8 us (14%)
    pallas_call x1, Pallas kernels, body(): pl.pallas_call(functools.partial(layer_kernel, sizes), out_shape=jax.Shap...  64 us
    unnamed x23, local copies, waits for them, and re-layouts  10.8 us

profile of v1, /device:TPU:6, one launch (start us, length us, event | category | flops | bytes accessed | tf_op | source)
XLA Modules:
  0.0 74.8 jit_solution(13911195522733539343)
XLA Ops:
  0.0 0.0 copy-start
  0.0 1.6 %copy-done = bf16[512,2048]{1,0:T(8,128)(2,1)S(1)} copy-done((bf16[512,2048]{1,0:T(8,128)(2,1)S(1)}, bf16[512,2048]{1,0:T(8,128)(2,1)}, u32[]{:S(2)}) %copy-start) | copy-done | bytes 2097176
  1.6 0.0 copy-start.1
  1.6 1.0 %copy-done.1 = bf16[512,512]{1,0:T(8,128)(2,1)S(1)} copy-done((bf16[512,512]{1,0:T(8,128)(2,1)S(1)}, bf16[512,512]{1,0:T(8,128)(2,1)}, u32[]{:S(2)}) %copy-start.1) | copy-done | bytes 524312
  2.6 0.0 copy-start.2
  2.6 1.0 %copy-done.2 = bf16[512,512]{1,0:T(8,128)(2,1)S(1)} copy-done((bf16[512,512]{1,0:T(8,128)(2,1)S(1)}, bf16[512,512]{1,0:T(8,128)(2,1)}, u32[]{:S(2)}) %copy-start.2) | copy-done | bytes 524312
  3.7 0.0 copy-start.3
  3.7 0.9 %copy-done.3 = bf16[512,128]{1,0:T(8,128)(2,1)S(1)} copy-done((bf16[512,128]{1,0:T(8,128)(2,1)S(1)}, bf16[512,128]{1,0:T(8,128)(2,1)}, u32[]{:S(2)}) %copy-start.3) | copy-done | bytes 131096
  4.6 0.0 copy-start.4
  4.6 0.9 %copy-done.4 = bf16[512,128]{1,0:T(8,128)(2,1)S(1)} copy-done((bf16[512,128]{1,0:T(8,128)(2,1)S(1)}, bf16[512,128]{1,0:T(8,128)(2,1)}, u32[]{:S(2)}) %copy-start.4) | copy-done | bytes 131096
  5.5 0.0 copy-start.5
  5.5 0.9 %copy-done.5 = bf16[512,128]{1,0:T(8,128)(2,1)S(1)} copy-done((bf16[512,128]{1,0:T(8,128)(2,1)S(1)}, bf16[512,128]{1,0:T(8,128)(2,1)}, u32[]{:S(2)}) %copy-start.5) | copy-done | bytes 131096
  6.4 0.0 copy-start.6
  6.4 0.9 %copy-done.6 = bf16[512,128]{1,0:T(8,128)(2,1)S(1)} copy-done((bf16[512,128]{1,0:T(8,128)(2,1)S(1)}, bf16[512,128]{1,0:T(8,128)(2,1)}, u32[]{:S(2)}) %copy-start.6) | copy-done | bytes 131096
  7.3 0.0 copy-start.7
  7.3 0.7 copy-done.7
  8.0 0.0 copy-start.8
  8.0 0.7 copy-done.8
  8.7 0.0 copy-start.9
  8.7 0.7 copy-done.9
  9.3 0.0 copy-start.10
  9.3 0.7 copy-done.10
  10.0 64.0 %layer.1 = bf16[128,2048]{1,0:T(8,128)(2,1)S(1)} custom-call(s32[2,2,8]{2,1,0:T(2,128)S(1)} %copy-done.7, f32[8]{0:T(128)S(1)} %copy-done.10, s32[4,128]{1,0:T(4,128)S(1)} %bitcast.2, f32[1,512]{1,0:T(1,128)S(1)} %bitcast.3, bf16[512,512]{1,0:T(8,128)(2,1)S(1)} %copy-done.1, bf16[512,512]{1,0:T(8,128)(2,1)S(1)} %copy-done.2, bf16[512,128]{1,0:T(8,128)(2,1)S(1)} %copy-done.3, ...), custom_call_target="tpu_custom_call" | custom-call | tf_op jit(solution)/shard_map/layer/pallas_call | solution.py:612
  74.0 0.8 %copy.13 = bf16[128,2048]{1,0:T(8,128)(2,1)} copy(bf16[128,2048]{1,0:T(8,128)(2,1)S(1)} %layer.1) | data formatting | bytes 1048576
Async XLA Ops:
  0.0 1.6 %copy-start = (bf16[512,2048]{1,0:T(8,128)(2,1)S(1)}, bf16[512,2048]{1,0:T(8,128)(2,1)}, u32[]{:S(2)}) copy-start(bf16[512,2048]{1,0:T(8,128)(2,1)} %w_hbm.1) | copy-start | bytes 6291460
  1.6 1.0 %copy-start.1 = (bf16[512,512]{1,0:T(8,128)(2,1)S(1)}, bf16[512,512]{1,0:T(8,128)(2,1)}, u32[]{:S(2)}) copy-start(bf16[512,512]{1,0:T(8,128)(2,1)} %acts_hbm.1) | copy-start | bytes 1572868
  2.6 1.0 %copy-start.2 = (bf16[512,512]{1,0:T(8,128)(2,1)S(1)}, bf16[512,512]{1,0:T(8,128)(2,1)}, u32[]{:S(2)}) copy-start(bf16[512,512]{1,0:T(8,128)(2,1)} %gate_hbm.1) | copy-start | bytes 1572868
  3.7 0.9 %copy-start.3 = (bf16[512,128]{1,0:T(8,128)(2,1)S(1)}, bf16[512,128]{1,0:T(8,128)(2,1)}, u32[]{:S(2)}) copy-start(bf16[512,128]{1,0:T(8,128)(2,1)} %fk_hbm.1) | copy-start | bytes 393220
  4.6 0.9 %copy-start.4 = (bf16[512,128]{1,0:T(8,128)(2,1)S(1)}, bf16[512,128]{1,0:T(8,128)(2,1)}, u32[]{:S(2)}) copy-start(bf16[512,128]{1,0:T(8,128)(2,1)} %fq_hbm.1) | copy-start | bytes 393220
  5.5 0.9 %copy-start.5 = (bf16[512,128]{1,0:T(8,128)(2,1)S(1)}, bf16[512,128]{1,0:T(8,128)(2,1)}, u32[]{:S(2)}) copy-start(bf16[512,128]{1,0:T(8,128)(2,1)} %bk_hbm.1) | copy-start | bytes 393220
  6.4 0.9 %copy-start.6 = (bf16[512,128]{1,0:T(8,128)(2,1)S(1)}, bf16[512,128]{1,0:T(8,128)(2,1)}, u32[]{:S(2)}) copy-start(bf16[512,128]{1,0:T(8,128)(2,1)} %bq_hbm.1) | copy-start | bytes 393220
  7.3 0.7 copy-start.7
  8.0 0.7 copy-start.8
  8.7 0.7 copy-start.9
  9.3 0.7 copy-start.10

commit v2 on v1

--- a/solution.py
+++ b/solution.py
@@ -13,6 +13,7 @@
 CH = 128
 HEAD = 64
 LANES = 128
+CUTS = 4
 SEQ = ("seq_0", "seq_1", "seq_2")
 MESH = pl.DeviceIdType.MESH
 F32 = jnp.float32
@@ -38,9 +39,14 @@
     return jnp.dot(a, b, preferred_element_type=F32)
 
 
-def chains(n_y):
+def chains(n_y, cuts):
     far, near = n_y // 2, n_y // 2 - 1
-    return ((1, 0, far), (-1, 1, far), (-1, 0, near), (1, 1, near))
+    out = []
+    for c in range(cuts):
+        up = far if c % 2 == 0 else near
+        out.append((1, c, up))
+        out.append((-1, c, far + near - up))
+    return [c for c in out if c[2] > 0]
 
 
 def layer_kernel(
@@ -117,7 +123,8 @@
     prow = states // n_p
     total_tokens = n_z * n_x * n_c * tokens
     dim = w_ref.shape[1]
-    half = dim // 2
+    cut_w = dim // CUTS
+    links = list(enumerate(chains(n_y, CUTS)))
     rows_out = tokens // POOL
     orow = rows_out // n_y
 
@@ -165,6 +172,13 @@
     ]
     for load in loads:
         load.start()
+    waited = set()
+
+    def need(n):
+        waited.add(n)
+        loads[n].wait()
+
+    sent = []
 
     low = lax.broadcasted_iota(jnp.int32, (1, LANES), 1) < HEAD
     logs, scal = [], []
@@ -210,7 +224,7 @@
         [jnp.exp(log_row[1][s] * step_f) * scal_row[1][s] for s in range(n_sp)],
     )
     for n in range(3):
-        loads[n].wait()
+        need(n)
 
     def chunk(a):
         return pl.ds(a * CH, CH)
@@ -263,7 +277,6 @@
             ),
         )
 
-    sent = []
     far_first = sorted(range(1, n_p), key=lambda k: -min(k // n_c, n_x - k // n_c))
     for k in far_first:
         for copy in p1_copies(k):
@@ -272,8 +285,8 @@
     recv1[me] = sbuf[me]
     recvp[me] = pbuf[...]
 
-    loads[3].wait()
-    loads[4].wait()
+    need(3)
+    need(4)
     apart = jnp.abs(rows - cols).astype(F32)
     left_m = jnp.where(low, 1.0, 0.0).astype(BF)
     right_m = jnp.where(low, 0.0, 1.0).astype(BF)
@@ -360,7 +373,7 @@
     recvz[iz] = jnp.zeros((prow, width), BF)
     recvzp[iz] = zpbuf[...]
 
-    loads[5].wait()
+    need(5)
     for a in range(n_ch):
         v = z_ref[chunk(a), :].astype(F32)
         silu_scr[chunk(a), :] = v / (1.0 + jnp.exp(-v))
@@ -454,15 +467,13 @@
     pooled = jnp.concatenate(pooled, axis=0)
     high = pooled.astype(BF)
     rest = (pooled - high.astype(F32)).astype(BF)
-    loads[6].wait()
+    need(6)
     for c in range(2):
-        cut = pl.ds(c * half, half)
+        cut = pl.ds(c * (dim // 2), dim // 2)
         w = w_ref[:, cut]
         result = dot(high, w) + dot(rest, w)
         for p in range(n_y):
             part[p, :, cut] = result[p * orow : (p + 1) * orow, :]
-
-    links = [c for c in enumerate(chains(n_y)) if c[1][2] > 0]
 
     def rs_copy(n, sign, s):
         return pltpu.make_async_remote_copy(
@@ -478,7 +489,7 @@
         for n, (sign, h, length) in links:
             if s >= length:
                 continue
-            cut = pl.ds(h * half, half)
+            cut = pl.ds(h * cut_w, cut_w)
             value = part[y_peer(sign * (length - s)), :, cut]
             if s > 0:
                 rs_copy(n, sign, s - 1).wait_recv()
@@ -491,18 +502,9 @@
     def out_rows(p):
         return pl.ds(pl.multiple_of(p * orow, orow), orow)
 
-    for h in range(2):
-        cut = pl.ds(h * half, half)
-        value = part[iy, :, cut]
-        for n, (sign, hh, length) in links:
-            if hh == h:
-                rs_copy(n, sign, length - 1).wait_recv()
-                value = value + rs_recv[n, length - 1].astype(F32)
-        obuf[out_rows(iy), cut] = value.astype(BF)
-
     def ag_copy(n, sign, h, s, own):
         p = y_peer(-sign * s) if own else y_peer(-sign * (s + 1))
-        view = obuf.at[out_rows(p), pl.ds(h * half, half)]
+        view = obuf.at[out_rows(p), pl.ds(h * cut_w, cut_w)]
         return pltpu.make_async_remote_copy(
             view,
             view,
@@ -512,15 +514,27 @@
             device_id_type=MESH,
         )
 
-    for s in range(n_y // 2):
+    def pass_on(n, sign, h, s):
+        copy = ag_copy(n, sign, h, s, True)
+        copy.start()
+        sent.append(copy)
+
+    for h in range(CUTS):
+        cut = pl.ds(h * cut_w, cut_w)
+        value = part[iy, :, cut]
+        for n, (sign, hh, length) in links:
+            if hh == h:
+                rs_copy(n, sign, length - 1).wait_recv()
+                value = value + rs_recv[n, length - 1].astype(F32)
+        obuf[out_rows(iy), cut] = value.astype(BF)
+        for n, (sign, hh, length) in links:
+            if hh == h:
+                pass_on(n, sign, h, 0)
+    for s in range(1, n_y // 2):
         for n, (sign, h, length) in links:
-            if s >= length:
-                continue
-            if s > 0:
+            if s < length:
                 ag_copy(n, sign, h, s - 1, False).wait_recv()
-            copy = ag_copy(n, sign, h, s, True)
-            copy.start()
-            sent.append(copy)
+                pass_on(n, sign, h, s)
     for n, (sign, h, length) in links:
         ag_copy(n, sign, h, length - 1, False).wait_recv()
     done = pltpu.make_async_copy(obuf, out_hbm, out_sem)
@@ -587,8 +601,8 @@
         vmem((n_ch, LANES), F32),
         vmem((n_y, n_ch, LANES), F32),
         vmem((n_y, orow, dim), F32),
-        vmem((4, steps, orow, dim // 2), BF),
-        vmem((4, steps, orow, dim // 2), BF),
+        vmem((2 * CUTS, steps, orow, dim // CUTS), BF),
+        vmem((2 * CUTS, steps, orow, dim // CUTS), BF),
         vmem((rows_out, dim), BF),
         dma((7,)),
         dma((n_p,)),
@@ -603,10 +617,10 @@
         dma((n_p,)),
         dma((n_y,)),
         dma((n_y,)),
-        dma((4, steps)),
-        dma((4, steps)),
-        dma((4, steps)),
-        dma((4, steps)),
+        dma((2 * CUTS, steps)),
+        dma((2 * CUTS, steps)),
+        dma((2 * CUTS, steps)),
+        dma((2 * CUTS, steps)),
         dma,
     ]
     return pl.pallas_call(
@@ -616,7 +630,7 @@
         out_specs=any_spec,
         scratch_shapes=scratch,
         compiler_params=pltpu.CompilerParams(
-            collective_id=0, has_side_effects=True, vmem_limit_bytes=40 << 20
+            collective_id=0, has_side_effects=True, vmem_limit_bytes=67043328
         ),
         name="layer",
     )(

time: 75.5 us -> 68.2 us (0.903)
  local copies, waits for them, and re-layouts: 10.8 us -> 1.88 us
  Pallas kernels: 64 us -> 65.6 us
    unnamed x23 -> x1, local copies, waits for them, and re-layouts: 10.8 us -> 1.88 us
    pallas_call x1, Pallas kernels: 64 us -> 65.6 us  [body(): pl.pallas_call(functools.partial(layer_kernel, sizes), out_shape=jax.Shap...]
where the time goes in v2:
time: 68.2 us; the launch traced here: 67.5 us
  Pallas kernels  65.6 us (96%)
  local copies, waits for them, and re-layouts  1.88 us (3%)
    pallas_call x1, Pallas kernels, body(): pl.pallas_call(functools.partial(layer_kernel, sizes), out_shape=jax.Shap...  65.6 us
    unnamed x1, local copies, waits for them, and re-layouts  1.88 us

profile of v2, /device:TPU:6, one launch (start us, length us, event | category | flops | bytes accessed | tf_op | source)
XLA Modules:
  0.0 67.5 jit_solution(13012572413341457254)
XLA Ops:
  0.0 65.6 %layer.1 = bf16[128,2048]{1,0:T(8,128)(2,1)} custom-call(s32[2,2,8]{2,1,0:T(2,128)} %codes_ref.1, f32[8]{0:T(128)} %skip_ref.1, s32[4,128]{1,0:T(4,128)} %bitcast.2, f32[1,512]{1,0:T(1,128)} %bitcast.3, bf16[512,512]{1,0:T(8,128)(2,1)} %acts_hbm.1, bf16[512,512]{1,0:T(8,128)(2,1)} %gate_hbm.1, bf16[512,128]{1,0:T(8,128)(2,1)} %fk_hbm.1, ...), custom_call_target="tpu_custom_call" | custom-call | tf_op jit(solution)/shard_map/layer/pallas_call | solution.py:626
  65.6 1.9 %copy.13 = bf16[128,2048]{1,0:T(8,128)(2,1)} copy(bf16[128,2048]{1,0:T(8,128)(2,1)} %layer.1) | data formatting | bytes 1048576

commit v3 on v2

--- a/solution.py
+++ b/solution.py
@@ -37,16 +37,6 @@
 
 def dot(a, b):
     return jnp.dot(a, b, preferred_element_type=F32)
-
-
-def chains(n_y, cuts):
-    far, near = n_y // 2, n_y // 2 - 1
-    out = []
-    for c in range(cuts):
-        up = far if c % 2 == 0 else near
-        out.append((1, c, up))
-        out.append((-1, c, far + near - up))
-    return [c for c in out if c[2] > 0]
 
 
 def layer_kernel(
@@ -124,7 +114,11 @@
     total_tokens = n_z * n_x * n_c * tokens
     dim = w_ref.shape[1]
     cut_w = dim // CUTS
-    links = list(enumerate(chains(n_y, CUTS)))
+    ways = [
+        (2 * h + i, sign, h, (sign == 1) == (h % 2 == 0))
+        for h in range(CUTS)
+        for i, sign in enumerate((1, -1))
+    ]
     rows_out = tokens // POOL
     orow = rows_out // n_y
 
@@ -144,17 +138,6 @@
 
     def y_peer(k, sign=1):
         return lax.rem(iy + sign * k + 2 * n_y, n_y)
-
-    barrier = pltpu.get_barrier_semaphore()
-    for k in range(1, n_p):
-        px, pc, _ = plane_peer(k)
-        pl.semaphore_signal(
-            barrier, inc=1, device_id={"seq_1": px, "seq_2": pc}, device_id_type=MESH
-        )
-    for k in range(1, n_z):
-        pl.semaphore_signal(barrier, inc=1, device_id={"seq_0": z_peer(k)}, device_id_type=MESH)
-    for k in range(1, n_y):
-        pl.semaphore_signal(barrier, inc=1, device_id={"chan": y_peer(k)}, device_id_type=MESH)
 
     loads = [
         pltpu.make_async_copy(src, dst, in_sem.at[n])
@@ -179,6 +162,17 @@
         loads[n].wait()
 
     sent = []
+
+    barrier = pltpu.get_barrier_semaphore()
+    for k in range(1, n_p):
+        px, pc, _ = plane_peer(k)
+        pl.semaphore_signal(
+            barrier, inc=1, device_id={"seq_1": px, "seq_2": pc}, device_id_type=MESH
+        )
+    for k in range(1, n_z):
+        pl.semaphore_signal(barrier, inc=1, device_id={"seq_0": z_peer(k)}, device_id_type=MESH)
+    for k in range(1, n_y):
+        pl.semaphore_signal(barrier, inc=1, device_id={"chan": y_peer(k)}, device_id_type=MESH)
 
     low = lax.broadcasted_iota(jnp.int32, (1, LANES), 1) < HEAD
     logs, scal = [], []
@@ -229,7 +223,6 @@
     def chunk(a):
         return pl.ds(a * CH, CH)
 
-    total_pass = []
     for d in range(2):
         keys_ref = (fk_ref, bk_ref)[d]
         mask = (last_m, first_m)[d]
@@ -253,35 +246,37 @@
 
     pl.semaphore_wait(barrier, (n_p - 1) + (n_z - 1) + (n_y - 1))
 
-    def p1_copies(k):
-        px, pc, pj = plane_peer(k)
-        where = {"seq_1": px, "seq_2": pc}
-        return (
-            pltpu.make_async_remote_copy(
-                pbuf, recvp.at[me], pps.at[k], ppr.at[k], device_id=where, device_id_type=MESH
-            ),
-            pltpu.make_async_remote_copy(
-                sbuf.at[pj], recv1.at[me], p1s.at[k], p1r.at[k], device_id=where, device_id_type=MESH
-            ),
-        )
-
-    def p1_arrivals(k):
-        px, pc, pj = plane_peer(k, -1)
-        where = {"seq_1": px, "seq_2": pc}
-        return (
-            pltpu.make_async_remote_copy(
-                pbuf, recvp.at[pj], pps.at[k], ppr.at[k], device_id=where, device_id_type=MESH
-            ),
-            pltpu.make_async_remote_copy(
-                sbuf.at[pj], recv1.at[pj], p1s.at[k], p1r.at[k], device_id=where, device_id_type=MESH
-            ),
-        )
+    def pp_copy(k, sign=1):
+        px, pc, pj = plane_peer(k, sign)
+        return pltpu.make_async_remote_copy(
+            pbuf,
+            recvp.at[me if sign == 1 else pj],
+            pps.at[k],
+            ppr.at[k],
+            device_id={"seq_1": px, "seq_2": pc},
+            device_id_type=MESH,
+        )
+
+    def p1_copy(k, sign=1):
+        px, pc, pj = plane_peer(k, sign)
+        return pltpu.make_async_remote_copy(
+            sbuf.at[pj],
+            recv1.at[me if sign == 1 else pj],
+            p1s.at[k],
+            p1r.at[k],
+            device_id={"seq_1": px, "seq_2": pc},
+            device_id_type=MESH,
+        )
+
+    def go(copy):
+        copy.start()
+        sent.append(copy)
 
     far_first = sorted(range(1, n_p), key=lambda k: -min(k // n_c, n_x - k // n_c))
     for k in far_first:
-        for copy in p1_copies(k):
-            copy.start()
-            sent.append(copy)
+        go(pp_copy(k))
+    for k in far_first:
+        go(p1_copy(k))
     recv1[me] = sbuf[me]
     recvp[me] = pbuf[...]
 
@@ -318,59 +313,38 @@
                 skip = jnp.where(low, skip_ref[2 * t], skip_ref[2 * t + 1])
                 y_scr[chunk(a), lanes] = dot(pair, both) + skip * xt.astype(F32)
 
-    for k in range(1, n_p):
-        for copy in p1_arrivals(k):
-            copy.wait_recv()
-
     def pass_row(ref, d):
         return jnp.concatenate(
             [ref[d * tiles + t : d * tiles + t + 1, :] for t in range(tiles)], axis=1
         )
 
+    def z_way(k, sign=1):
+        pz = z_peer(k, sign)
+        return pz, iz if sign == 1 else pz
+
+    def zp_copy(k, sign=1):
+        pz, slot = z_way(k, sign)
+        return pltpu.make_async_remote_copy(
+            zpbuf,
+            recvzp.at[slot],
+            zps.at[k],
+            zpr.at[k],
+            device_id={"seq_0": pz},
+            device_id_type=MESH,
+        )
+
+    z_far_first = sorted(range(1, n_z), key=lambda k: -min(k, n_z - k))
+    for k in range(1, n_p):
+        pp_copy(k, -1).wait_recv()
     for d in range(2):
-        order = range(n_p) if d == 0 else range(n_p - 1, -1, -1)
-        state = jnp.zeros((prow, width), F32)
         through = jnp.ones((1, width), F32)
-        for q in order:
-            a_scr[d, q] = state
+        for q in range(n_p) if d == 0 else range(n_p - 1, -1, -1):
             q_scr[d, q] = jnp.broadcast_to(through, (8, width))
-            factor = pass_row(recvp.at[q], d)
-            state = factor * state + recv1[q, d].astype(F32)
-            through = factor * through
-        zbuf[d] = state.astype(BF)
+            through = pass_row(recvp.at[q], d) * through
         for t in range(tiles):
             zpbuf[d * tiles + t : d * tiles + t + 1, :] = through[:, t * LANES : (t + 1) * LANES]
-
-    def z_copies(k):
-        pz = z_peer(k)
-        where = {"seq_0": pz}
-        d = jnp.where(pz > iz, 0, 1)
-        return (
-            pltpu.make_async_remote_copy(
-                zpbuf, recvzp.at[iz], zps.at[k], zpr.at[k], device_id=where, device_id_type=MESH
-            ),
-            pltpu.make_async_remote_copy(
-                zbuf.at[d], recvz.at[iz], zs.at[k], zr.at[k], device_id=where, device_id_type=MESH
-            ),
-        )
-
-    def z_arrivals(k):
-        pz = z_peer(k, -1)
-        where = {"seq_0": pz}
-        return (
-            pltpu.make_async_remote_copy(
-                zpbuf, recvzp.at[pz], zps.at[k], zpr.at[k], device_id=where, device_id_type=MESH
-            ),
-            pltpu.make_async_remote_copy(
-                zbuf.at[0], recvz.at[pz], zs.at[k], zr.at[k], device_id=where, device_id_type=MESH
-            ),
-        )
-
-    for k in sorted(range(1, n_z), key=lambda k: -min(k, n_z - k)):
-        for copy in z_copies(k):
-            copy.start()
-            sent.append(copy)
-    recvz[iz] = jnp.zeros((prow, width), BF)
+    for k in z_far_first:
+        go(zp_copy(k))
     recvzp[iz] = zpbuf[...]
 
     need(5)
@@ -381,9 +355,35 @@
         cw_scr[0, s] = jnp.exp(log_row[0][s] * (step_f + 1.0))
         cw_scr[1, s] = jnp.exp(log_row[1][s] * (float(CH) - step_f))
 
+    for k in range(1, n_p):
+        p1_copy(k, -1).wait_recv()
+
+    for d in range(2):
+        order = range(n_p) if d == 0 else range(n_p - 1, -1, -1)
+        state = jnp.zeros((prow, width), F32)
+        for q in order:
+            a_scr[d, q] = state
+            state = pass_row(recvp.at[q], d) * state + recv1[q, d].astype(F32)
+        zbuf[d] = state.astype(BF)
+
+    def z_copy(k, sign=1):
+        pz, slot = z_way(k, sign)
+        return pltpu.make_async_remote_copy(
+            zbuf.at[jnp.where(pz > iz, 0, 1)],
+            recvz.at[slot],
+            zs.at[k],
+            zr.at[k],
+            device_id={"seq_0": pz},
+            device_id_type=MESH,
+        )
+
+    for k in z_far_first:
+        go(z_copy(k))
+    recvz[iz] = jnp.zeros((prow, width), BF)
+
     for k in range(1, n_z):
-        for copy in z_arrivals(k):
-            copy.wait_recv()
+        zp_copy(k, -1).wait_recv()
+        z_copy(k, -1).wait_recv()
 
     for d in range(2):
         state = jnp.zeros((prow, width), F32)
@@ -405,9 +405,7 @@
         )
 
     for k in far_first:
-        copy = p3_copy(k)
-        copy.start()
-        sent.append(copy)
+        go(p3_copy(k))
     recv3[me] = ebuf[me]
     for k in range(1, n_p):
         p3_copy(k, -1).wait_recv()
@@ -440,9 +438,7 @@
         )
 
     for k in sorted(range(1, n_y), key=lambda k: -min(k, n_y - k)):
-        copy = q_copy(k)
-        copy.start()
-        sent.append(copy)
+        go(q_copy(k))
     recvq[iy] = qbuf[...]
     for k in range(1, n_y):
         q_copy(k, -1).wait_recv()
@@ -465,78 +461,84 @@
         hidden = (y_scr[chunk(a), :] * inv_full * gain).astype(BF)
         pooled.append(dot(pool, hidden))
     pooled = jnp.concatenate(pooled, axis=0)
-    high = pooled.astype(BF)
-    rest = (pooled - high.astype(F32)).astype(BF)
+    pooled = pooled.astype(BF)
     need(6)
     for c in range(2):
         cut = pl.ds(c * (dim // 2), dim // 2)
         w = w_ref[:, cut]
-        result = dot(high, w) + dot(rest, w)
+        result = dot(pooled, w)
         for p in range(n_y):
             part[p, :, cut] = result[p * orow : (p + 1) * orow, :]
 
-    def rs_copy(n, sign, s):
-        return pltpu.make_async_remote_copy(
-            rs_send.at[n, s],
-            rs_recv.at[n, s],
-            rss.at[n, s],
-            rsr.at[n, s],
-            device_id={"chan": y_peer(sign)},
-            device_id_type=MESH,
-        )
-
-    for s in range(n_y // 2):
-        for n, (sign, h, length) in links:
-            if s >= length:
-                continue
-            cut = pl.ds(h * cut_w, cut_w)
-            value = part[y_peer(sign * (length - s)), :, cut]
-            if s > 0:
-                rs_copy(n, sign, s - 1).wait_recv()
-                value = value + rs_recv[n, s - 1].astype(F32)
-            rs_send[n, s] = value.astype(BF)
-            copy = rs_copy(n, sign, s)
-            copy.start()
-            sent.append(copy)
-
-    def out_rows(p):
-        return pl.ds(pl.multiple_of(p * orow, orow), orow)
-
-    def ag_copy(n, sign, h, s, own):
-        p = y_peer(-sign * s) if own else y_peer(-sign * (s + 1))
-        view = obuf.at[out_rows(p), pl.ds(h * cut_w, cut_w)]
+    def lanes_of(h):
+        return pl.ds(h * cut_w, cut_w)
+
+    def rs_copy(n, slot, sign, hops):
+        return pltpu.make_async_remote_copy(
+            rs_send.at[n, slot],
+            rs_recv.at[n, slot],
+            rss.at[n, slot],
+            rsr.at[n, slot],
+            device_id={"chan": y_peer(sign * hops)},
+            device_id_type=MESH,
+        )
+
+    def send_part(n, slot, sign, h, away, hops):
+        rs_send[n, slot] = part[y_peer(sign * away), :, lanes_of(h)].astype(BF)
+        go(rs_copy(n, slot, sign, hops))
+
+    for n, sign, h, far in ways:
+        if far:
+            send_part(n, 0, sign, h, 4, 2)
+    for n, sign, h, far in ways:
+        send_part(n, 1, sign, h, 3, 1)
+    for n, sign, h, far in ways:
+        send_part(n, 2, sign, h, 1, 1)
+    for n, sign, h, far in ways:
+        value = part[y_peer(2 * sign), :, lanes_of(h)]
+        rs_copy(n, 1, sign, 1).wait_recv()
+        value = value + rs_recv[n, 1].astype(F32)
+        if far:
+            rs_copy(n, 0, sign, 2).wait_recv()
+            value = value + rs_recv[n, 0].astype(F32)
+        rs_send[n, 3] = value.astype(BF)
+        go(rs_copy(n, 3, sign, 2))
+
+    def ag_copy(n, slot, sign, h, hops, rows_from):
+        p = pl.multiple_of(y_peer(rows_from) * orow, orow)
+        view = obuf.at[pl.ds(p, orow), lanes_of(h)]
         return pltpu.make_async_remote_copy(
             view,
             view,
-            ags.at[n, s],
-            agr.at[n, s],
-            device_id={"chan": y_peer(sign)},
-            device_id_type=MESH,
-        )
-
-    def pass_on(n, sign, h, s):
-        copy = ag_copy(n, sign, h, s, True)
-        copy.start()
-        sent.append(copy)
+            ags.at[n, slot],
+            agr.at[n, slot],
+            device_id={"chan": y_peer(sign * hops)},
+            device_id_type=MESH,
+        )
 
     for h in range(CUTS):
-        cut = pl.ds(h * cut_w, cut_w)
-        value = part[iy, :, cut]
-        for n, (sign, hh, length) in links:
+        value = part[iy, :, lanes_of(h)]
+        for n, sign, hh, far in ways:
             if hh == h:
-                rs_copy(n, sign, length - 1).wait_recv()
-                value = value + rs_recv[n, length - 1].astype(F32)
-        obuf[out_rows(iy), cut] = value.astype(BF)
-        for n, (sign, hh, length) in links:
+                rs_copy(n, 2, sign, 1).wait_recv()
+                value = value + rs_recv[n, 2].astype(F32)
+                rs_copy(n, 3, sign, 2).wait_recv()
+                value = value + rs_recv[n, 3].astype(F32)
+        obuf[pl.ds(pl.multiple_of(iy * orow, orow), orow), lanes_of(h)] = value.astype(BF)
+        for n, sign, hh, far in ways:
             if hh == h:
-                pass_on(n, sign, h, 0)
-    for s in range(1, n_y // 2):
-        for n, (sign, h, length) in links:
-            if s < length:
-                ag_copy(n, sign, h, s - 1, False).wait_recv()
-                pass_on(n, sign, h, s)
-    for n, (sign, h, length) in links:
-        ag_copy(n, sign, h, length - 1, False).wait_recv()
+                go(ag_copy(n, 0, sign, h, 2, 0))
+                go(ag_copy(n, 1, sign, h, 1, 0))
+    for n, sign, h, far in ways:
+        ag_copy(n, 0, sign, h, 2, -2 * sign).wait_recv()
+        if far:
+            go(ag_copy(n, 3, sign, h, 2, -2 * sign))
+        go(ag_copy(n, 2, sign, h, 1, -2 * sign))
+    for n, sign, h, far in ways:
+        ag_copy(n, 1, sign, h, 1, -sign).wait_recv()
+        ag_copy(n, 2, sign, h, 1, -3 * sign).wait_recv()
+        if far:
+            ag_copy(n, 3, sign, h, 2, -4 * sign).wait_recv()
     done = pltpu.make_async_copy(obuf, out_hbm, out_sem)
     done.start()
     for copy in sent:
@@ -567,7 +569,7 @@
     prow = states // n_p
     rows_out = tokens // POOL
     orow = rows_out // n_y
-    steps = n_y // 2
+    steps = 4
     vmem = pltpu.VMEM
     dma = pltpu.SemaphoreType.DMA
     any_spec = pl.BlockSpec(memory_space=pl.ANY)

time: 68.2 us -> 59.4 us (0.87)
  Pallas kernels: 65.6 us -> 56.8 us
    pallas_call x1, Pallas kernels: 65.6 us -> 56.8 us  [body(): pl.pallas_call(functools.partial(layer_kernel, sizes), out_shape=jax.Shap...]
where the time goes in v3:
time: 59.4 us; the launch traced here: 58.7 us
  Pallas kernels  56.8 us (96%)
  local copies, waits for them, and re-layouts  1.88 us (3%)
    pallas_call x1, Pallas kernels, body(): pl.pallas_call(functools.partial(layer_kernel, sizes), out_shape=jax.Shap...  56.8 us
    unnamed x1, local copies, waits for them, and re-layouts  1.88 us

profile of v3, /device:TPU:6, one launch (start us, length us, event | category | flops | bytes accessed | tf_op | source)
XLA Modules:
  0.0 58.7 jit_solution(7733040337720020169)
XLA Ops:
  0.0 56.8 %layer.1 = bf16[128,2048]{1,0:T(8,128)(2,1)} custom-call(s32[2,2,8]{2,1,0:T(2,128)} %codes_ref.1, f32[8]{0:T(128)} %skip_ref.1, s32[4,128]{1,0:T(4,128)} %bitcast.2, f32[1,512]{1,0:T(1,128)} %bitcast.3, bf16[512,512]{1,0:T(8,128)(2,1)} %acts_hbm.1, bf16[512,512]{1,0:T(8,128)(2,1)} %gate_hbm.1, bf16[512,128]{1,0:T(8,128)(2,1)} %fk_hbm.1, ...), custom_call_target="tpu_custom_call" | custom-call | tf_op jit(solution)/shard_map/layer/pallas_call | solution.py:628
  56.8 1.9 %copy.13 = bf16[128,2048]{1,0:T(8,128)(2,1)} copy(bf16[128,2048]{1,0:T(8,128)(2,1)} %layer.1) | data formatting | bytes 1048576

commit v4 on v3

--- a/solution.py
+++ b/solution.py
@@ -41,10 +41,10 @@
 
 def layer_kernel(
     sizes,
-    codes_ref,
-    skip_ref,
-    clip_ref,
-    gain_ref,
+    codes_hbm,
+    skip_hbm,
+    clip_hbm,
+    gain_hbm,
     acts_hbm,
     gate_hbm,
     fk_hbm,
@@ -52,7 +52,11 @@
     bk_hbm,
     bq_hbm,
     w_hbm,
-    out_hbm,
+    out_ref,
+    codes_ref,
+    skip_ref,
+    clip_ref,
+    gain_ref,
     x_ref,
     z_ref,
     fk_ref,
@@ -143,23 +147,26 @@
         pltpu.make_async_copy(src, dst, in_sem.at[n])
         for n, (src, dst) in enumerate(
             (
+                (codes_hbm, codes_ref),
+                (clip_hbm, clip_ref),
                 (acts_hbm, x_ref),
                 (fk_hbm, fk_ref),
                 (bk_hbm, bk_ref),
                 (fq_hbm, fq_ref),
                 (bq_hbm, bq_ref),
+                (skip_hbm, skip_ref),
                 (gate_hbm, z_ref),
+                (gain_hbm, gain_ref),
                 (w_hbm, w_ref),
             )
         )
     ]
-    for load in loads:
+    for load in loads[:5]:
         load.start()
-    waited = set()
-
-    def need(n):
-        waited.add(n)
-        loads[n].wait()
+
+    def need(*which):
+        for n in which:
+            loads[n].wait()
 
     sent = []
 
@@ -174,6 +181,7 @@
     for k in range(1, n_y):
         pl.semaphore_signal(barrier, inc=1, device_id={"chan": y_peer(k)}, device_id_type=MESH)
 
+    need(0, 1)
     low = lax.broadcasted_iota(jnp.int32, (1, LANES), 1) < HEAD
     logs, scal = [], []
     for d in range(2):
@@ -217,8 +225,9 @@
         [jnp.exp(log_row[0][s] * (CH - 1.0 - step_f)) * scal_row[0][s] for s in range(n_sp)],
         [jnp.exp(log_row[1][s] * step_f) * scal_row[1][s] for s in range(n_sp)],
     )
-    for n in range(3):
-        need(n)
+    need(2, 3, 4)
+    for load in loads[5:9]:
+        load.start()
 
     def chunk(a):
         return pl.ds(a * CH, CH)
@@ -280,8 +289,9 @@
     recv1[me] = sbuf[me]
     recvp[me] = pbuf[...]
 
-    need(3)
-    need(4)
+    need(5, 6, 7)
+    for load in loads[9:]:
+        load.start()
     apart = jnp.abs(rows - cols).astype(F32)
     left_m = jnp.where(low, 1.0, 0.0).astype(BF)
     right_m = jnp.where(low, 0.0, 1.0).astype(BF)
@@ -347,7 +357,7 @@
         go(zp_copy(k))
     recvzp[iz] = zpbuf[...]
 
-    need(5)
+    need(8)
     for a in range(n_ch):
         v = z_ref[chunk(a), :].astype(F32)
         silu_scr[chunk(a), :] = v / (1.0 + jnp.exp(-v))
@@ -453,6 +463,7 @@
         1.0 / POOL,
         0.0,
     ).astype(BF)
+    need(9)
     gain = gain_ref[...]
     pooled = []
     for a in range(n_ch):
@@ -462,7 +473,7 @@
         pooled.append(dot(pool, hidden))
     pooled = jnp.concatenate(pooled, axis=0)
     pooled = pooled.astype(BF)
-    need(6)
+    need(10)
     for c in range(2):
         cut = pl.ds(c * (dim // 2), dim // 2)
         w = w_ref[:, cut]
@@ -506,9 +517,9 @@
 
     def ag_copy(n, slot, sign, h, hops, rows_from):
         p = pl.multiple_of(y_peer(rows_from) * orow, orow)
-        view = obuf.at[pl.ds(p, orow), lanes_of(h)]
-        return pltpu.make_async_remote_copy(
-            view,
+        view = out_ref.at[pl.ds(p, orow), lanes_of(h)]
+        return pltpu.make_async_remote_copy(
+            obuf.at[:, lanes_of(h)] if rows_from == 0 else view,
             view,
             ags.at[n, slot],
             agr.at[n, slot],
@@ -524,11 +535,15 @@
                 value = value + rs_recv[n, 2].astype(F32)
                 rs_copy(n, 3, sign, 2).wait_recv()
                 value = value + rs_recv[n, 3].astype(F32)
-        obuf[pl.ds(pl.multiple_of(iy * orow, orow), orow), lanes_of(h)] = value.astype(BF)
+        obuf[:, lanes_of(h)] = value.astype(BF)
         for n, sign, hh, far in ways:
             if hh == h:
                 go(ag_copy(n, 0, sign, h, 2, 0))
                 go(ag_copy(n, 1, sign, h, 1, 0))
+    done = pltpu.make_async_copy(
+        obuf, out_ref.at[pl.ds(pl.multiple_of(iy * orow, orow), orow), :], out_sem
+    )
+    done.start()
     for n, sign, h, far in ways:
         ag_copy(n, 0, sign, h, 2, -2 * sign).wait_recv()
         if far:
@@ -539,11 +554,9 @@
         ag_copy(n, 2, sign, h, 1, -3 * sign).wait_recv()
         if far:
             ag_copy(n, 3, sign, h, 2, -4 * sign).wait_recv()
-    done = pltpu.make_async_copy(obuf, out_hbm, out_sem)
-    done.start()
+    done.wait()
     for copy in sent:
         copy.wait_send()
-    done.wait()
 
 
 def body(
@@ -572,10 +585,11 @@
     steps = 4
     vmem = pltpu.VMEM
     dma = pltpu.SemaphoreType.DMA
-    any_spec = pl.BlockSpec(memory_space=pl.ANY)
-    smem_spec = pl.BlockSpec(memory_space=pltpu.SMEM)
-    vmem_spec = pl.BlockSpec(memory_space=pltpu.VMEM)
     scratch = [
+        pltpu.SMEM(decay_codes.shape, jnp.int32),
+        pltpu.SMEM(skip_gain.shape, F32),
+        vmem((n_ch, CH), jnp.int32),
+        vmem((1, width), F32),
         vmem((tokens, width), BF),
         vmem((tokens, width), BF),
         vmem((tokens, states), BF),
@@ -605,8 +619,8 @@
         vmem((n_y, orow, dim), F32),
         vmem((2 * CUTS, steps, orow, dim // CUTS), BF),
         vmem((2 * CUTS, steps, orow, dim // CUTS), BF),
-        vmem((rows_out, dim), BF),
-        dma((7,)),
+        vmem((orow, dim), BF),
+        dma((11,)),
         dma((n_p,)),
         dma((n_p,)),
         dma((n_p,)),
@@ -628,14 +642,14 @@
     return pl.pallas_call(
         functools.partial(layer_kernel, sizes),
         out_shape=jax.ShapeDtypeStruct((rows_out, dim), BF),
-        in_specs=[smem_spec, smem_spec, vmem_spec, vmem_spec] + [any_spec] * 7,
-        out_specs=any_spec,
+        in_specs=[pl.BlockSpec(memory_space=pltpu.HBM)] * 11,
+        out_specs=pl.BlockSpec(memory_space=pl.ANY),
         scratch_shapes=scratch,
         compiler_params=pltpu.CompilerParams(
-            collective_id=0, has_side_effects=True, vmem_limit_bytes=67043328
+            collective_id=0, has_side_effects=True, vmem_limit_bytes=40 << 20
         ),
         name="layer",
-    )(
+    )(*(pltpu.with_memory_space_constraint(v, pltpu.HBM) for v in (
         decay_codes,
         skip_gain,
         clip_start.reshape(n_ch, CH),
@@ -647,7 +661,7 @@
         backward_keys,
         backward_queries,
         out_weight,
-    )
+    )))
 
 
 def solution(mesh):

time: 59.4 us -> 56.9 us (0.958)
  Pallas kernels: 56.8 us -> 55.5 us
  local copies, waits for them, and re-layouts: 1.88 us -> 0.8 us
    pallas_call x1, Pallas kernels: 56.8 us -> 55.5 us  [body(): pl.pallas_call(functools.partial(layer_kernel, sizes), out_shape=jax.Shap...]
    unnamed x1, local copies, waits for them, and re-layouts: 1.88 us -> 0.8 us
where the time goes in v4:
time: 56.9 us; the launch traced here: 56.3 us
  Pallas kernels  55.5 us (98%)
  local copies, waits for them, and re-layouts  0.8 us (1%)
    pallas_call x1, Pallas kernels, body(): pl.pallas_call(functools.partial(layer_kernel, sizes), out_shape=jax.Shap...  55.5 us

profile of v4, /device:TPU:6, one launch (start us, length us, event | category | flops | bytes accessed | tf_op | source)
XLA Modules:
  0.0 56.3 jit_solution(14320954949909832287)
XLA Ops:
  0.0 55.5 %layer.1 = bf16[128,2048]{1,0:T(8,128)(2,1)S(1)} custom-call(s32[2,2,8]{2,1,0:T(2,128)} %codes_hbm.1, f32[8]{0:T(128)} %skip_hbm.1, s32[4,128]{1,0:T(4,128)} %bitcast.2, f32[1,512]{1,0:T(1,128)} %bitcast.3, bf16[512,512]{1,0:T(8,128)(2,1)} %acts_hbm.1, bf16[512,512]{1,0:T(8,128)(2,1)} %gate_hbm.1, bf16[512,128]{1,0:T(8,128)(2,1)} %fk_hbm.1, ...), custom_call_target="tpu_custom_call" | custom-call | tf_op jit(solution)/shard_map/layer/pallas_call | solution.py:642
  55.5 0.8 %copy.13 = bf16[128,2048]{1,0:T(8,128)(2,1)} copy(bf16[128,2048]{1,0:T(8,128)(2,1)S(1)} %layer.1) | data formatting | bytes 1048576

commit v5 on v4

--- a/solution.py
+++ b/solution.py
@@ -232,27 +232,29 @@
     def chunk(a):
         return pl.ds(a * CH, CH)
 
+    through = [[None] * n_ch, [None] * n_ch]
     for d in range(2):
+        left = jnp.ones((1, width), F32)
+        for a in range(n_ch) if d == 0 else range(n_ch - 1, -1, -1):
+            through[d][a] = left
+            left = passing[d][a] * left
+        for t in range(tiles):
+            pbuf[d * tiles + t : d * tiles + t + 1, :] = left[:, t * LANES : (t + 1) * LANES]
+
+    def own_states(d):
         keys_ref = (fk_ref, bk_ref)[d]
         mask = (last_m, first_m)[d]
-        order = range(n_ch) if d == 0 else range(n_ch - 1, -1, -1)
-        state, through = None, None
-        for a in order:
-            if state is None:
-                st_scr[d, a] = jnp.zeros((states, width), F32)
-                carry_scr[d, a] = jnp.ones((8, width), F32)
-            else:
+        state = None
+        for a in range(n_ch) if d == 0 else range(n_ch - 1, -1, -1):
+            if state is not None:
                 st_scr[d, a] = state
-                carry_scr[d, a] = jnp.broadcast_to(through, (8, width))
             scaled = (x_ref[chunk(a), :].astype(F32) * (grow[d][a * CH // SPAN] * mask[a])).astype(BF)
             local = dot_t(keys_ref[chunk(a), :], scaled)
             state = local if state is None else passing[d][a] * state + local
-            through = passing[d][a] if through is None else passing[d][a] * through
         for j in range(n_p):
             sbuf[j, d] = state[j * prow : (j + 1) * prow, :].astype(BF)
-        for t in range(tiles):
-            pbuf[d * tiles + t : d * tiles + t + 1, :] = through[:, t * LANES : (t + 1) * LANES]
-
+
+    own_states(0)
     pl.semaphore_wait(barrier, (n_p - 1) + (n_z - 1) + (n_y - 1))
 
     def pp_copy(k, sign=1):
@@ -266,13 +268,13 @@
             device_id_type=MESH,
         )
 
-    def p1_copy(k, sign=1):
+    def p1_copy(d, k, sign=1):
         px, pc, pj = plane_peer(k, sign)
         return pltpu.make_async_remote_copy(
-            sbuf.at[pj],
-            recv1.at[me if sign == 1 else pj],
-            p1s.at[k],
-            p1r.at[k],
+            sbuf.at[pj, d],
+            recv1.at[me if sign == 1 else pj, d],
+            p1s.at[d, k],
+            p1r.at[d, k],
             device_id={"seq_1": px, "seq_2": pc},
             device_id_type=MESH,
         )
@@ -285,7 +287,10 @@
     for k in far_first:
         go(pp_copy(k))
     for k in far_first:
-        go(p1_copy(k))
+        go(p1_copy(0, k))
+    own_states(1)
+    for k in far_first:
+        go(p1_copy(1, k))
     recv1[me] = sbuf[me]
     recvp[me] = pbuf[...]
 
@@ -347,12 +352,12 @@
     for k in range(1, n_p):
         pp_copy(k, -1).wait_recv()
     for d in range(2):
-        through = jnp.ones((1, width), F32)
+        left = jnp.ones((1, width), F32)
         for q in range(n_p) if d == 0 else range(n_p - 1, -1, -1):
-            q_scr[d, q] = jnp.broadcast_to(through, (8, width))
-            through = pass_row(recvp.at[q], d) * through
+            q_scr[d, q] = jnp.broadcast_to(left, (8, width))
+            left = pass_row(recvp.at[q], d) * left
         for t in range(tiles):
-            zpbuf[d * tiles + t : d * tiles + t + 1, :] = through[:, t * LANES : (t + 1) * LANES]
+            zpbuf[d * tiles + t : d * tiles + t + 1, :] = left[:, t * LANES : (t + 1) * LANES]
     for k in z_far_first:
         go(zp_copy(k))
     recvzp[iz] = zpbuf[...]
@@ -365,8 +370,9 @@
         cw_scr[0, s] = jnp.exp(log_row[0][s] * (step_f + 1.0))
         cw_scr[1, s] = jnp.exp(log_row[1][s] * (float(CH) - step_f))
 
-    for k in range(1, n_p):
-        p1_copy(k, -1).wait_recv()
+    for d in range(2):
+        for k in range(1, n_p):
+            p1_copy(d, k, -1).wait_recv()
 
     for d in range(2):
         order = range(n_p) if d == 0 else range(n_p - 1, -1, -1)
@@ -391,6 +397,20 @@
         go(z_copy(k))
     recvz[iz] = jnp.zeros((prow, width), BF)
 
+    for a in range(n_ch):
+        silu = silu_scr[chunk(a), :]
+        local = y_scr[chunk(a), :]
+        for d in range(2):
+            first = a == (0 if d == 0 else n_ch - 1)
+            reach = cw_scr[d, a * CH // SPAN] * (first_m, last_m)[d][a]
+            if first:
+                carry_scr[d, a] = reach * silu
+            else:
+                queries = (fq_ref, bq_ref)[d][chunk(a), :]
+                local = local + reach * dot(queries, st_scr[d, a].astype(BF))
+                carry_scr[d, a] = reach * silu * through[d][a]
+        y_scr[chunk(a), :] = local * silu
+
     for k in range(1, n_z):
         zp_copy(k, -1).wait_recv()
         z_copy(k, -1).wait_recv()
@@ -421,14 +441,10 @@
         p3_copy(k, -1).wait_recv()
 
     for a in range(n_ch):
-        s = a * CH // SPAN
+        gated = y_scr[chunk(a), :]
         for d in range(2):
-            entering = jnp.concatenate([recv3[q, d] for q in range(n_p)], axis=0).astype(F32)
-            state = st_scr[d, a] + carry_scr[d, a][0:1, :] * entering
-            mask = (first_m, last_m)[d]
-            queries = (fq_ref, bq_ref)[d][chunk(a), :]
-            y_scr[chunk(a), :] += (cw_scr[d, s] * mask[a]) * dot(queries, state.astype(BF))
-        gated = y_scr[chunk(a), :] * silu_scr[chunk(a), :]
+            entering = jnp.concatenate([recv3[q, d] for q in range(n_p)], axis=0)
+            gated = gated + carry_scr[d, a] * dot((fq_ref, bq_ref)[d][chunk(a), :], entering)
         y_scr[chunk(a), :] = gated
         squares = gated * gated
         lanes_sum = squares[:, :LANES]
@@ -450,6 +466,10 @@
     for k in sorted(range(1, n_y), key=lambda k: -min(k, n_y - k)):
         go(q_copy(k))
     recvq[iy] = qbuf[...]
+    need(9)
+    gain = gain_ref[...]
+    for a in range(n_ch):
+        y_scr[chunk(a), :] = y_scr[chunk(a), :] * gain
     for k in range(1, n_y):
         q_copy(k, -1).wait_recv()
     squares = recvq[0]
@@ -463,24 +483,14 @@
         1.0 / POOL,
         0.0,
     ).astype(BF)
-    need(9)
-    gain = gain_ref[...]
     pooled = []
     for a in range(n_ch):
         inv_col = jnp.broadcast_to(inv[a : a + 1, :], (CH, LANES)).T
         inv_full = jnp.concatenate([inv_col] * tiles, axis=1)
-        hidden = (y_scr[chunk(a), :] * inv_full * gain).astype(BF)
+        hidden = (y_scr[chunk(a), :] * inv_full).astype(BF)
         pooled.append(dot(pool, hidden))
     pooled = jnp.concatenate(pooled, axis=0)
     pooled = pooled.astype(BF)
-    need(10)
-    for c in range(2):
-        cut = pl.ds(c * (dim // 2), dim // 2)
-        w = w_ref[:, cut]
-        result = dot(pooled, w)
-        for p in range(n_y):
-            part[p, :, cut] = result[p * orow : (p + 1) * orow, :]
-
     def lanes_of(h):
         return pl.ds(h * cut_w, cut_w)
 
@@ -498,11 +508,18 @@
         rs_send[n, slot] = part[y_peer(sign * away), :, lanes_of(h)].astype(BF)
         go(rs_copy(n, slot, sign, hops))
 
-    for n, sign, h, far in ways:
-        if far:
-            send_part(n, 0, sign, h, 4, 2)
-    for n, sign, h, far in ways:
-        send_part(n, 1, sign, h, 3, 1)
+    need(10)
+    for c in range(2):
+        cut = pl.ds(c * (dim // 2), dim // 2)
+        result = dot(pooled, w_ref[:, cut])
+        for p in range(n_y):
+            part[p, :, cut] = result[p * orow : (p + 1) * orow, :]
+        mine = [way for way in ways if way[2] * 2 // CUTS == c]
+        for n, sign, h, far in mine:
+            if far:
+                send_part(n, 0, sign, h, 4, 2)
+        for n, sign, h, far in mine:
+            send_part(n, 1, sign, h, 3, 1)
     for n, sign, h, far in ways:
         send_part(n, 2, sign, h, 1, 1)
     for n, sign, h, far in ways:
@@ -600,7 +617,7 @@
         vmem((tokens, width), F32),
         vmem((tokens, width), F32),
         vmem((2, n_ch, states, width), F32),
-        vmem((2, n_ch, 8, width), F32),
+        vmem((2, n_ch, CH, width), F32),
         vmem((2, n_sp, CH, width), F32),
         vmem((n_p, 2, prow, width), BF),
         vmem((n_p, 2, prow, width), BF),
@@ -621,8 +638,8 @@
         vmem((2 * CUTS, steps, orow, dim // CUTS), BF),
         vmem((orow, dim), BF),
         dma((11,)),
-        dma((n_p,)),
-        dma((n_p,)),
+        dma((2, n_p)),
+        dma((2, n_p)),
         dma((n_p,)),
         dma((n_p,)),
         dma((n_z,)),

time: 56.9 us -> 56.5 us (level)
  no operation moved by 1% of the time
where the time goes in v5:
time: 56.5 us; the launch traced here: 56.4 us
  Pallas kernels  55.6 us (98%)
  local copies, waits for them, and re-layouts  0.8 us (1%)
    pallas_call x1, Pallas kernels, body(): pl.pallas_call(functools.partial(layer_kernel, sizes), out_shape=jax.Shap...  55.6 us

profile of v5, /device:TPU:6, one launch (start us, length us, event | category | flops | bytes accessed | tf_op | source)
XLA Modules:
  0.0 56.4 jit_solution(4981681659614046171)
XLA Ops:
  0.0 55.6 %layer.1 = bf16[128,2048]{1,0:T(8,128)(2,1)S(1)} custom-call(s32[2,2,8]{2,1,0:T(2,128)} %codes_hbm.1, f32[8]{0:T(128)} %skip_hbm.1, s32[4,128]{1,0:T(4,128)} %bitcast.2, f32[1,512]{1,0:T(1,128)} %bitcast.3, bf16[512,512]{1,0:T(8,128)(2,1)} %acts_hbm.1, bf16[512,512]{1,0:T(8,128)(2,1)} %gate_hbm.1, bf16[512,128]{1,0:T(8,128)(2,1)} %fk_hbm.1, ...), custom_call_target="tpu_custom_call" | custom-call | tf_op jit(solution)/shard_map/layer/pallas_call | solution.py:659
  55.6 0.8 %copy.13 = bf16[128,2048]{1,0:T(8,128)(2,1)} copy(bf16[128,2048]{1,0:T(8,128)(2,1)S(1)} %layer.1) | data formatting | bytes 1048576

commit v6 on v5

--- a/solution.py
+++ b/solution.py
@@ -170,6 +170,10 @@
 
     sent = []
 
+    for d in range(2):
+        for q in range(n_z):
+            recvz[d, q] = jnp.zeros((prow, width), BF)
+
     barrier = pltpu.get_barrier_semaphore()
     for k in range(1, n_p):
         px, pc, _ = plane_peer(k)
@@ -254,7 +258,7 @@
         for j in range(n_p):
             sbuf[j, d] = state[j * prow : (j + 1) * prow, :].astype(BF)
 
-    own_states(0)
+    own_states(1)
     pl.semaphore_wait(barrier, (n_p - 1) + (n_z - 1) + (n_y - 1))
 
     def pp_copy(k, sign=1):
@@ -287,10 +291,10 @@
     for k in far_first:
         go(pp_copy(k))
     for k in far_first:
+        go(p1_copy(1, k))
+    own_states(0)
+    for k in far_first:
         go(p1_copy(0, k))
-    own_states(1)
-    for k in far_first:
-        go(p1_copy(1, k))
     recv1[me] = sbuf[me]
     recvp[me] = pbuf[...]
 
@@ -370,32 +374,43 @@
         cw_scr[0, s] = jnp.exp(log_row[0][s] * (step_f + 1.0))
         cw_scr[1, s] = jnp.exp(log_row[1][s] * (float(CH) - step_f))
 
-    for d in range(2):
-        for k in range(1, n_p):
-            p1_copy(d, k, -1).wait_recv()
-
-    for d in range(2):
-        order = range(n_p) if d == 0 else range(n_p - 1, -1, -1)
-        state = jnp.zeros((prow, width), F32)
-        for q in order:
-            a_scr[d, q] = state
-            state = pass_row(recvp.at[q], d) * state + recv1[q, d].astype(F32)
-        zbuf[d] = state.astype(BF)
-
-    def z_copy(k, sign=1):
+    def z_copy(d, k, sign=1):
         pz, slot = z_way(k, sign)
         return pltpu.make_async_remote_copy(
-            zbuf.at[jnp.where(pz > iz, 0, 1)],
-            recvz.at[slot],
+            zbuf.at[d],
+            recvz.at[d, slot],
             zs.at[k],
             zr.at[k],
             device_id={"seq_0": pz},
             device_id_type=MESH,
         )
 
-    for k in z_far_first:
-        go(z_copy(k))
-    recvz[iz] = jnp.zeros((prow, width), BF)
+    def above(q):
+        return q > iz
+
+    def below(q):
+        return q < iz
+
+    def send_total(d, k):
+        @pl.when((above, below)[d](z_peer(k)))
+        def _():
+            z_copy(d, k).start()
+
+    def total_arrived(d, k):
+        @pl.when((below, above)[d](z_peer(k, -1)))
+        def _():
+            z_copy(d, k, -1).wait_recv()
+
+    for d in (1, 0):
+        for k in range(1, n_p):
+            p1_copy(d, k, -1).wait_recv()
+        state = jnp.zeros((prow, width), F32)
+        for q in range(n_p) if d == 0 else range(n_p - 1, -1, -1):
+            a_scr[d, q] = state
+            state = pass_row(recvp.at[q], d) * state + recv1[q, d].astype(F32)
+        zbuf[d] = state.astype(BF)
+        for k in z_far_first:
+            send_total(d, k)
 
     for a in range(n_ch):
         silu = silu_scr[chunk(a), :]
@@ -411,40 +426,44 @@
                 carry_scr[d, a] = reach * silu * through[d][a]
         y_scr[chunk(a), :] = local * silu
 
+    def p3_copy(d, k, sign=1):
+        px, pc, pj = plane_peer(k, sign)
+        return pltpu.make_async_remote_copy(
+            ebuf.at[pj, d],
+            recv3.at[me if sign == 1 else pj, d],
+            p3s.at[d, k],
+            p3r.at[d, k],
+            device_id={"seq_1": px, "seq_2": pc},
+            device_id_type=MESH,
+        )
+
     for k in range(1, n_z):
         zp_copy(k, -1).wait_recv()
-        z_copy(k, -1).wait_recv()
-
-    for d in range(2):
+    for d in (1, 0):
+        for k in range(1, n_z):
+            total_arrived(d, k)
         state = jnp.zeros((prow, width), F32)
         for q in range(n_z) if d == 0 else range(n_z - 1, -1, -1):
-            new = pass_row(recvzp.at[q], d) * state + recvz[q].astype(F32)
-            state = jnp.where(q < iz if d == 0 else q > iz, new, state)
+            new = pass_row(recvzp.at[q], d) * state + recvz[d, q].astype(F32)
+            state = jnp.where((below, above)[d](q), new, state)
         for q in range(n_p):
             ebuf[q, d] = (a_scr[d, q] + q_scr[d, q][0:1, :] * state).astype(BF)
-
-    def p3_copy(k, sign=1):
-        px, pc, pj = plane_peer(k, sign)
-        return pltpu.make_async_remote_copy(
-            ebuf.at[pj],
-            recv3.at[me if sign == 1 else pj],
-            p3s.at[k],
-            p3r.at[k],
-            device_id={"seq_1": px, "seq_2": pc},
-            device_id_type=MESH,
-        )
-
-    for k in far_first:
-        go(p3_copy(k))
-    recv3[me] = ebuf[me]
+        for k in far_first:
+            go(p3_copy(d, k))
+        recv3[me, d] = ebuf[me, d]
+
+    def entering_part(d, a):
+        entering = jnp.concatenate([recv3[q, d] for q in range(n_p)], axis=0)
+        return carry_scr[d, a] * dot((fq_ref, bq_ref)[d][chunk(a), :], entering)
+
     for k in range(1, n_p):
-        p3_copy(k, -1).wait_recv()
-
+        p3_copy(1, k, -1).wait_recv()
     for a in range(n_ch):
-        gated = y_scr[chunk(a), :]
-        for d in range(2):
-            entering = jnp.concatenate([recv3[q, d] for q in range(n_p)], axis=0)
-            gated = gated + carry_scr[d, a] * dot((fq_ref, bq_ref)[d][chunk(a), :], entering)
+        y_scr[chunk(a), :] += entering_part(1, a)
+    for k in range(1, n_p):
+        p3_copy(0, k, -1).wait_recv()
+    for a in range(n_ch):
+        gated = y_scr[chunk(a), :] + entering_part(0, a)
         y_scr[chunk(a), :] = gated
         squares = gated * gated
         lanes_sum = squares[:, :LANES]
@@ -572,6 +591,8 @@
         if far:
             ag_copy(n, 3, sign, h, 2, -4 * sign).wait_recv()
     done.wait()
+    for k in range(1, n_z):
+        z_copy(0, k).wait_send()
     for copy in sent:
         copy.wait_send()
 
@@ -626,7 +647,7 @@
         vmem((2, n_p, prow, width), F32),
         vmem((2, n_p, 8, width), F32),
         vmem((2, prow, width), BF),
-        vmem((n_z, prow, width), BF),
+        vmem((2, n_z, prow, width), BF),
         vmem((8, LANES), F32),
         vmem((n_z, 8, LANES), F32),
         vmem((n_p, 2, prow, width), BF),
@@ -646,8 +667,8 @@
         dma((n_z,)),
         dma((n_z,)),
         dma((n_z,)),
-        dma((n_p,)),
-        dma((n_p,)),
+        dma((2, n_p)),
+        dma((2, n_p)),
         dma((n_y,)),
         dma((n_y,)),
         dma((2 * CUTS, steps)),

time: 56.5 us -> 56 us (level)
  Pallas kernels: 55.6 us -> 54.7 us
    pallas_call x1, Pallas kernels: 55.6 us -> 54.7 us  [body(): pl.pallas_call(functools.partial(layer_kernel, sizes), out_shape=jax.Shap...]
where the time goes in v6:
time: 56 us; the launch traced here: 55.5 us
  Pallas kernels  54.7 us (98%)
  local copies, waits for them, and re-layouts  0.8 us (1%)
    pallas_call x1, Pallas kernels, body(): pl.pallas_call(functools.partial(layer_kernel, sizes), out_shape=jax.Shap...  54.7 us

profile of v6, /device:TPU:6, one launch (start us, length us, event | category | flops | bytes accessed | tf_op | source)
XLA Modules:
  0.0 55.5 jit_solution(16577836696383074502)
XLA Ops:
  0.0 54.7 %layer.1 = bf16[128,2048]{1,0:T(8,128)(2,1)S(1)} custom-call(s32[2,2,8]{2,1,0:T(2,128)} %codes_hbm.1, f32[8]{0:T(128)} %skip_hbm.1, s32[4,128]{1,0:T(4,128)} %bitcast.2, f32[1,512]{1,0:T(1,128)} %bitcast.3, bf16[512,512]{1,0:T(8,128)(2,1)} %acts_hbm.1, bf16[512,512]{1,0:T(8,128)(2,1)} %gate_hbm.1, bf16[512,128]{1,0:T(8,128)(2,1)} %fk_hbm.1, ...), custom_call_target="tpu_custom_call" | custom-call | tf_op jit(solution)/shard_map/layer/pallas_call | solution.py:680
  54.7 0.8 %copy.13 = bf16[128,2048]{1,0:T(8,128)(2,1)} copy(bf16[128,2048]{1,0:T(8,128)(2,1)S(1)} %layer.1) | data formatting | bytes 1048576

commit v7 on v6

--- a/solution.py
+++ b/solution.py
@@ -13,7 +13,7 @@
 CH = 128
 HEAD = 64
 LANES = 128
-CUTS = 4
+CUTS = 2
 SEQ = ("seq_0", "seq_1", "seq_2")
 MESH = pl.DeviceIdType.MESH
 F32 = jnp.float32
@@ -225,10 +225,12 @@
     ]
 
     step_f = lax.broadcasted_iota(jnp.int32, (CH, width), 0).astype(F32)
-    grow = (
-        [jnp.exp(log_row[0][s] * (CH - 1.0 - step_f)) * scal_row[0][s] for s in range(n_sp)],
-        [jnp.exp(log_row[1][s] * step_f) * scal_row[1][s] for s in range(n_sp)],
-    )
+
+    def growth(d):
+        steps = CH - 1.0 - step_f if d == 0 else step_f
+        return [jnp.exp(log_row[d][s] * steps) * scal_row[d][s] for s in range(n_sp)]
+
+    grow = {1: growth(1)}
     need(2, 3, 4)
     for load in loads[5:9]:
         load.start()
@@ -292,6 +294,7 @@
         go(pp_copy(k))
     for k in far_first:
         go(p1_copy(1, k))
+    grow[0] = growth(0)
     own_states(0)
     for k in far_first:
         go(p1_copy(0, k))
@@ -366,14 +369,6 @@
         go(zp_copy(k))
     recvzp[iz] = zpbuf[...]
 
-    need(8)
-    for a in range(n_ch):
-        v = z_ref[chunk(a), :].astype(F32)
-        silu_scr[chunk(a), :] = v / (1.0 + jnp.exp(-v))
-    for s in range(n_sp):
-        cw_scr[0, s] = jnp.exp(log_row[0][s] * (step_f + 1.0))
-        cw_scr[1, s] = jnp.exp(log_row[1][s] * (float(CH) - step_f))
-
     def z_copy(d, k, sign=1):
         pz, slot = z_way(k, sign)
         return pltpu.make_async_remote_copy(
@@ -411,6 +406,14 @@
         zbuf[d] = state.astype(BF)
         for k in z_far_first:
             send_total(d, k)
+
+    need(8)
+    for a in range(n_ch):
+        v = z_ref[chunk(a), :].astype(F32)
+        silu_scr[chunk(a), :] = v / (1.0 + jnp.exp(-v))
+    for s in range(n_sp):
+        cw_scr[0, s] = jnp.exp(log_row[0][s] * (step_f + 1.0))
+        cw_scr[1, s] = jnp.exp(log_row[1][s] * (float(CH) - step_f))
 
     for a in range(n_ch):
         silu = silu_scr[chunk(a), :]

time: 56 us -> 55.8 us (level)
  no operation moved by 1% of the time
where the time goes in v7:
time: 55.8 us; the launch traced here: 55.3 us
  Pallas kernels  54.5 us (98%)
  local copies, waits for them, and re-layouts  0.8 us (1%)
    pallas_call x1, Pallas kernels, body(): pl.pallas_call(functools.partial(layer_kernel, sizes), out_shape=jax.Shap...  54.5 us

profile of v7, /device:TPU:6, one launch (start us, length us, event | category | flops | bytes accessed | tf_op | source)
XLA Modules:
  0.0 55.3 jit_solution(11855112081343217002)
XLA Ops:
  0.0 54.5 %layer.1 = bf16[128,2048]{1,0:T(8,128)(2,1)S(1)} custom-call(s32[2,2,8]{2,1,0:T(2,128)} %codes_hbm.1, f32[8]{0:T(128)} %skip_hbm.1, s32[4,128]{1,0:T(4,128)} %bitcast.2, f32[1,512]{1,0:T(1,128)} %bitcast.3, bf16[512,512]{1,0:T(8,128)(2,1)} %acts_hbm.1, bf16[512,512]{1,0:T(8,128)(2,1)} %gate_hbm.1, bf16[512,128]{1,0:T(8,128)(2,1)} %fk_hbm.1, ...), custom_call_target="tpu_custom_call" | custom-call | tf_op jit(solution)/shard_map/layer/pallas_call | solution.py:683
  54.5 0.8 %copy.13 = bf16[128,2048]{1,0:T(8,128)(2,1)} copy(bf16[128,2048]{1,0:T(8,128)(2,1)S(1)} %layer.1) | data formatting | bytes 1048576

commit v8 on v7

--- a/solution.py
+++ b/solution.py
@@ -578,7 +578,8 @@
         for n, sign, hh, far in ways:
             if hh == h:
                 go(ag_copy(n, 0, sign, h, 2, 0))
-                go(ag_copy(n, 1, sign, h, 1, 0))
+    for n, sign, h, far in ways:
+        go(ag_copy(n, 1, sign, h, 1, 0))
     done = pltpu.make_async_copy(
         obuf, out_ref.at[pl.ds(pl.multiple_of(iy * orow, orow), orow), :], out_sem
     )

time: 55.8 us -> 55.9 us (level)
  no operation moved by 1% of the time
where the time goes in v8:
time: 55.9 us; the launch traced here: 55.3 us
  Pallas kernels  54.5 us (97%)
  local copies, waits for them, and re-layouts  0.8 us (1%)
    pallas_call x1, Pallas kernels, body(): pl.pallas_call(functools.partial(layer_kernel, sizes), out_shape=jax.Shap...  54.5 us

profile of v8, /device:TPU:6, one launch (start us, length us, event | category | flops | bytes accessed | tf_op | source)
XLA Modules:
  0.0 55.3 jit_solution(11729358020026573760)
XLA Ops:
  0.0 54.5 %layer.1 = bf16[128,2048]{1,0:T(8,128)(2,1)S(1)} custom-call(s32[2,2,8]{2,1,0:T(2,128)} %codes_hbm.1, f32[8]{0:T(128)} %skip_hbm.1, s32[4,128]{1,0:T(4,128)} %bitcast.2, f32[1,512]{1,0:T(1,128)} %bitcast.3, bf16[512,512]{1,0:T(8,128)(2,1)} %acts_hbm.1, bf16[512,512]{1,0:T(8,128)(2,1)} %gate_hbm.1, bf16[512,128]{1,0:T(8,128)(2,1)} %fk_hbm.1, ...), custom_call_target="tpu_custom_call" | custom-call | tf_op jit(solution)/shard_map/layer/pallas_call | solution.py:684
  54.5 0.8 %copy.13 = bf16[128,2048]{1,0:T(8,128)(2,1)} copy(bf16[128,2048]{1,0:T(8,128)(2,1)S(1)} %layer.1) | data formatting | bytes 1048576
